TPU v7x, 256 devices: a whole 4x4x8 slice. The times are simulated.
256 devices in a mesh: expert: 64 (over z, x_lo, y), dp: 4 (over x_hi, core).
Axes of the slice: x: 4 (x_hi: 2, x_lo: 2; x = x_hi * 2 + x_lo), y: 4, z: 8, core: 2. Of those that a mesh axis runs over, the one named last changes fastest.
Arguments:
- tokens: bfloat16 [8192, 3584], P('expert', 'dp'), may hold values from -6 to 6
- expert_ids: int32 [8192, 8], P('expert'), may hold values from 0 to 127, as said below
- gate_weights: float32 [8192, 8], P('expert'), may hold values from 0.05 to 0.5
- replica_plan: int32 [64], replicated, may hold values from 0 to 127, as said below
- w_gate: bfloat16 [128, 3584, 1024], P('expert', None, 'dp'), may hold values from -0.09375 to 0.09375
- w_up: bfloat16 [128, 3584, 1024], P('expert', None, 'dp'), may hold values from -0.09375 to 0.09375
- w_down: bfloat16 [128, 1024, 3584], P('expert', 'dp'), may hold values from -0.1875 to 0.1875
Outputs:
- mixed_out: bfloat16 [8192, 3584], P('expert', 'dp')
Inputs may be any that keep to these rules, and one draw needn't show every extreme that they name: `expert_ids`: each row names 8 different experts; one expert, which varies with the draw, is named by every row. `replica_plan`: entry j names one of the 2 experts owned by index (j + 32) % 64 of the expert axis, that is, an expert from k * 2 to k * 2 + 1 with that index k.
All inputs are finite; a program needn't handle non-finite values.
Results may differ from a plain program's by a relative error of at most 0.012.
Values may be sent and summed in bfloat16 or wider, within the bound.
A program may use at most 128 MiB of HBM per device.

v0:
```python
import jax
import jax.numpy as jnp
from jax import lax
from jax.sharding import PartitionSpec as P

CAP = 8


def passed_along(value, axis, steps):
    count = lax.axis_size(axis)
    pairs = [(source, (source + steps) % count) for source in range(count)]
    return lax.ppermute(value, axis, pairs)


def expert_block(slot_rows, gate_piece, up_piece, down_piece):
    gate_value = jnp.dot(slot_rows, gate_piece, preferred_element_type=jnp.float32)
    up_value = jnp.dot(slot_rows, up_piece, preferred_element_type=jnp.float32)
    hidden = (jax.nn.silu(gate_value) * up_value).astype(jnp.bfloat16)
    return jnp.dot(hidden, down_piece, preferred_element_type=jnp.float32).astype(jnp.bfloat16)


def per_device(tokens, expert_ids, gate_weights, replica_plan, w_gate, w_up, w_down):
    owners = lax.axis_size("expert")
    own_index = lax.axis_index("expert")
    owned_count = w_gate.shape[0]
    host_slots = owned_count + 1
    experts = owned_count * owners
    tok_rows = tokens.shape[0]
    choose_count = expert_ids.shape[1]
    feature_share = tokens.shape[1]
    model_width = feature_share * lax.axis_size("dp")
    flat_ids = expert_ids.reshape(-1)
    assigned = flat_ids.shape[0]
    expert_range = jnp.arange(experts, dtype=jnp.int32)
    onehot = (flat_ids[:, None] == expert_range[None, :]).astype(jnp.int32)
    earlier = jnp.cumsum(onehot, axis=0) - onehot
    row_rank = jnp.sum(earlier * onehot, axis=1)
    hosted = (replica_plan[:, None] == expert_range[None, :]).astype(jnp.int32)
    copies = 1 + jnp.sum(hosted, axis=0)
    host_of = jnp.sum(jnp.arange(owners, dtype=jnp.int32)[:, None] * hosted, axis=0)
    my_copies = jnp.sum(onehot * copies[None, :], axis=1)
    my_host = jnp.sum(onehot * host_of[None, :], axis=1)
    copy_index = row_rank % my_copies
    position = row_rank // my_copies
    is_kept = position < CAP
    target = jnp.where(copy_index == 0, flat_ids // owned_count, my_host)
    target_slot = jnp.where(copy_index == 0, flat_ids % owned_count, owned_count)
    buffer_rows = owners * host_slots * CAP
    slot_place = jnp.where(
        is_kept, (target * host_slots + target_slot) * CAP + position, buffer_rows
    )
    token_of = jnp.arange(assigned, dtype=jnp.int32) // choose_count
    source = jnp.full((buffer_rows,), tok_rows, jnp.int32).at[slot_place].set(token_of, mode="drop")
    half_way = owners // 2
    receiver = (own_index + half_way) % owners
    local_pick = replica_plan[receiver] - own_index * owned_count
    outgoing_weights = (
        lax.dynamic_index_in_dim(w_gate, local_pick, 0, keepdims=False),
        lax.dynamic_index_in_dim(w_up, local_pick, 0, keepdims=False),
        lax.dynamic_index_in_dim(w_down, local_pick, 0, keepdims=False),
    )
    features = lax.all_gather(tokens, "dp", axis=1, tiled=True)
    padded = jnp.concatenate([features, jnp.zeros((1, model_width), jnp.bfloat16)], axis=0)
    outgoing = padded[source].reshape(owners, host_slots * CAP, model_width)
    arrived = lax.all_to_all(outgoing, "expert", split_axis=0, concat_axis=0, tiled=True)
    arrived = arrived.reshape(owners, host_slots, CAP, model_width)
    guest_gate, guest_up, guest_down = passed_along(
        (outgoing_weights[0], outgoing_weights[1], outgoing_weights[2]), "expert", half_way
    )
    results = []
    for slot_number in range(host_slots):
        slot_rows = arrived[:, slot_number].reshape(owners * CAP, model_width)
        if slot_number < owned_count:
            block_out = expert_block(
                slot_rows, w_gate[slot_number], w_up[slot_number], w_down[slot_number]
            )
        else:
            block_out = expert_block(slot_rows, guest_gate, guest_up, guest_down)
        results.append(block_out.reshape(owners, CAP, model_width))
    partials = jnp.stack(results, axis=1).reshape(owners, host_slots * CAP, model_width)
    weights_kept = jnp.where(is_kept, gate_weights.reshape(-1), 0.0)
    lookup = jnp.minimum(slot_place, buffer_rows - 1)
    returned = lax.all_to_all(partials, "expert", split_axis=0, concat_axis=0, tiled=True).reshape(
        buffer_rows, model_width
    )
    picked = returned[lookup].astype(jnp.float32) * weights_kept[:, None]
    combined = jnp.sum(picked.reshape(tok_rows, choose_count, model_width), axis=1)
    mixed_out = lax.psum_scatter(
        combined.astype(jnp.bfloat16), "dp", scatter_dimension=1, tiled=True
    )
    return mixed_out


def solution(mesh):
    in_specs = (
        P("expert", "dp"),
        P("expert", None),
        P("expert", None),
        P(),
        P("expert", None, "dp"),
        P("expert", None, "dp"),
        P("expert", "dp", None),
    )
    out_specs = P("expert", "dp")
    return jax.shard_map(
        per_device, mesh=mesh, in_specs=in_specs, out_specs=out_specs, check_vma=False
    )
```

profile of v0, /device:TPU:2, one launch (start us, length us, event | category | flops | bytes accessed | tf_op | source)
XLA Modules:
  0.0 900.7 jit_solution(2319679141427596992)
XLA Ops:
  6.5 0.0 copy-start.3
  6.5 0.8 copy.42
  7.4 0.1 eq.76
  7.5 0.1 eq.72
  7.5 0.1 reshape.306
  7.7 0.1 copy.44
  7.8 0.2 fusion.50
  8.1 0.1 copy.45
  8.2 0.7 select_reduce_fusion.2
  8.9 0.6 select_reduce_fusion
  9.6 0.7 compare_select_fusion
  10.3 4.3 scatter_custom_fusion
  14.7 0.0 copy-done.3
  14.7 10.4 %all_gather.3 = bf16[128,3584]{1,0:T(8,128)(2,1)S(1)} all-gather(bf16[128,896]{1,0:T(8,128)(2,1)S(1)} %copy-done.3), channel_id=1, replica_groups=mesh['expert'=64,'dp'=4] {'dp'}, dimensions={1}, use_global_device_ids=true | all-gather | bytes 1146880 | tf_op jit(solution)/shard_map/all_gather | solution.py:62
  25.1 0.1 concatenate.3
  25.1 9.1 %gather_fusion = bf16[1536,3584]{1,0:T(8,128)(2,1)} fusion(bf16[129,3584]{1,0:T(8,128)(2,1)S(1)} %concatenate.3, s32[2048]{0:T(1024)S(1)} %pad_clamp_fusion), kind=kCustom, calls=%fused_computation | custom fusion | bytes 22026240 | tf_op jit(solution)/shard_map/gather | solution.py:64
  34.2 0.0 copy-start.5
  34.2 13.4 %all-to-all-start = ((bf16[64,24,3584]{2,1,0:T(8,128)(2,1)}), bf16[64,24,3584]{2,1,0:T(8,128)(2,1)}, u32[]{:S(2)}, u32[]{:S(2)}) async-start(bf16[64,24,3584]{2,1,0:T(8,128)(2,1)} %bitcast.105), calls=%async_computation | async-start | bytes 22020096 | tf_op jit(solution)/shard_map/all_to_all | solution.py:65
  47.7 0.0 copy-done.5
  47.7 0.6 dynamic_slice.14
  48.9 0.0 copy-start
  49.0 0.0 copy-start.2
  49.0 3.0 dynamic-slice_bitcast_fusion.1
  51.9 5.5 collective-permute-start.1
  57.4 0.0 copy-done
  57.4 0.1 dynamic-slice_bitcast_fusion.2
  57.6 0.5 collective-permute-start
  58.1 0.0 copy-done.2
  58.1 1.4 dynamic-slice_bitcast_fusion
  59.5 5.5 collective-permute-start.2
  65.0 347.3 %all-to-all-done = bf16[64,24,3584]{2,1,0:T(8,128)(2,1)} async-done(((bf16[64,24,3584]{2,1,0:T(8,128)(2,1)}), bf16[64,24,3584]{2,1,0:T(8,128)(2,1)}, u32[]{:S(2)}, u32[]{:S(2)}) %all-to-all-start) | async-done | bytes 11010080 | tf_op jit(solution)/shard_map/all_to_all | solution.py:65
  412.3 0.0 copy-start.1
  412.3 3.9 fusion.5
  416.2 0.0 copy-done.1
  416.2 3.1 fusion.7
  419.3 0.0 collective-permute-done.1
  419.3 3.7 fusion.8
  423.1 8.9 fusion.1
  431.9 9.0 fusion.2
  440.9 0.0 collective-permute-done
  440.9 0.0 collective-permute-done.2
  440.9 8.9 fusion.3
  449.9 10.2 %maximum_bitcast_fusion = bf16[64,24,3584]{2,1,0:T(8,128)(2,1)} fusion(bf16[64,1,8,3584]{3,2,1,0:T(8,128)(2,1)} %fusion.3, bf16[64,1,8,3584]{3,2,1,0:T(8,128)(2,1)} %fusion.2, bf16[64,1,8,3584]{3,2,1,0:T(8,128)(2,1)} %fusion.1), kind=kLoop, calls=%fused_computation.5 | loop fusion | flops 11010048 | bytes 22020096 | tf_op jit(solution)/shard_map/reshape | solution.py:80
  460.0 0.0 copy-start.4
  460.0 125.9 %all-to-all-start.1 = ((bf16[64,24,3584]{2,1,0:T(8,128)(2,1)}), bf16[64,24,3584]{2,1,0:T(8,128)(2,1)}, u32[]{:S(2)}, u32[]{:S(2)}) async-start(bf16[64,24,3584]{2,1,0:T(8,128)(2,1)} %maximum_bitcast_fusion), calls=%async_computation.1 | async-start | bytes 22020096 | tf_op jit(solution)/shard_map/all_to_all | solution.py:83
  585.9 0.3 reduce-scatter.4.cloned.1.call-start
  586.2 0.1 div.58
  586.3 0.1 div.59
  586.4 0.1 fusion.63
  586.6 0.1 and.101
  586.7 0.1 copy.51
  586.8 0.0 copy-done.4
  586.8 0.1 copy.53
  586.9 240.1 %all-to-all-done.1 = bf16[64,24,3584]{2,1,0:T(8,128)(2,1)} async-done(((bf16[64,24,3584]{2,1,0:T(8,128)(2,1)}), bf16[64,24,3584]{2,1,0:T(8,128)(2,1)}, u32[]{:S(2)}, u32[]{:S(2)}) %all-to-all-start.1) | async-done | bytes 11010080 | tf_op jit(solution)/shard_map/all_to_all | solution.py:83
  827.0 19.3 %gather_fusion.1 = bf16[1024,3584]{1,0:T(8,128)(2,1)} fusion(bf16[1536,3584]{1,0:T(8,128)(2,1)} %bitcast.29, s32[1024]{0:T(1024)S(1)} %broadcast_clamp_fusion), kind=kCustom, calls=%fused_computation.1 | custom fusion | bytes 14684160 | tf_op jit(solution)/shard_map/gather | solution.py:86
  846.4 9.8 %fusion = bf16[128,3584]{1,0:T(8,128)(2,1)S(1)} fusion(bf16[1024,3584]{1,0:T(8,128)(2,1)} %gather_fusion.1, f32[128,8]{1,0:T(8,128)S(1)} %copy.53), kind=kLoop, calls=%fused_computation.4 | loop fusion | flops 10551296 | bytes 8261632 | tf_op jit(solution)/shard_map/reduce_sum | solution.py:87
  856.2 1.3 copy.54
  857.5 0.0 reduce-scatter.4.cloned.1.call-update
  857.5 34.6 %reduce-scatter.4.cloned.1.call-done = bf16[896,128]{1,0:T(8,128)(2,1)} async-done(((bf16[3584,128]{1,0:T(8,128)(2,1)}), bf16[896,128]{1,0:T(8,128)(2,1)}) %reduce-scatter.4.cloned.1.call-update) | async-done | bytes 229392
  892.0 1.8 copy.55
  (12 shorter events, 0.2 us)
Async XLA Ops:
  6.5 8.1 copy-start.3
  34.2 13.4 %copy-start.5 = (s32[64]{0:T(128)S(1)}, s32[64]{0:T(128)}, u32[]{:S(2)}) copy-start(s32[64]{0:T(128)} %param.10) | copy-start | bytes 772
  34.2 378.1 %all-to-all-start = ((bf16[64,24,3584]{2,1,0:T(8,128)(2,1)}), bf16[64,24,3584]{2,1,0:T(8,128)(2,1)}, u32[]{:S(2)}, u32[]{:S(2)}) async-start(bf16[64,24,3584]{2,1,0:T(8,128)(2,1)} %bitcast.105), calls=%async_computation | async-start | bytes 22020096 | tf_op jit(solution)/shard_map/all_to_all | solution.py:65
  48.9 8.5 copy-start
  49.0 9.1 %copy-start.2 = (bf16[2,256,3584]{2,1,0:T(8,128)(2,1)S(1)}, bf16[2,256,3584]{2,1,0:T(8,128)(2,1)}, u32[]{:S(2)}) copy-start(bf16[2,256,3584]{2,1,0:T(8,128)(2,1)} %param.13) | copy-start | bytes 11010052
  51.9 367.4 %collective-permute-start.1 = (bf16[3584,256]{1,0:T(8,128)(2,1)}, bf16[3584,256]{1,0:T(8,128)(2,1)}, u32[]{:S(2)}, u32[]{:S(2)}) collective-permute-start(bf16[3584,256]{1,0:T(8,128)(2,1)} %dynamic-slice_bitcast_fusion.1), channel_id=1, source_target_pairs={{0,128},{4,132},{8,136},{12,140},{16,144},{20,148},{24,152},{28,15... | collective-permute-start | bytes 5505032 | tf_op jit(solution)/shard_map/ppermute | solution.py:12
  57.6 383.4 %collective-permute-start = (bf16[3584,256]{1,0:T(8,128)(2,1)S(1)}, bf16[3584,256]{1,0:T(8,128)(2,1)}, u32[]{:S(2)}, u32[]{:S(2)}) collective-permute-start(bf16[3584,256]{1,0:T(8,128)(2,1)S(1)} %dynamic-slice_bitcast_fusion.2), channel_id=1, source_target_pairs={{0,128},{4,132},{8,136},{12,140},{16,144},{20,148},{24,152},{28,15... | collective-permute-start | bytes 5505032 | tf_op jit(solution)/shard_map/ppermute | solution.py:12
  59.5 381.5 %collective-permute-start.2 = (bf16[256,3584]{1,0:T(8,128)(2,1)}, bf16[256,3584]{1,0:T(8,128)(2,1)}, u32[]{:S(2)}, u32[]{:S(2)}) collective-permute-start(bf16[256,3584]{1,0:T(8,128)(2,1)} %dynamic-slice_bitcast_fusion), channel_id=1, source_target_pairs={{0,128},{4,132},{8,136},{12,140},{16,144},{20,148},{24,152},{28,15... | collective-permute-start | bytes 5505032 | tf_op jit(solution)/shard_map/ppermute | solution.py:12
  412.3 3.9 copy-start.1
  460.0 126.7 %copy-start.4 = (f32[128,8]{0,1:T(8,128)S(1)}, f32[128,8]{0,1:T(8,128)}, u32[]{:S(2)}) copy-start(f32[128,8]{0,1:T(8,128)} %param.9) | copy-start | bytes 12292
  460.0 367.0 %all-to-all-start.1 = ((bf16[64,24,3584]{2,1,0:T(8,128)(2,1)}), bf16[64,24,3584]{2,1,0:T(8,128)(2,1)}, u32[]{:S(2)}, u32[]{:S(2)}) async-start(bf16[64,24,3584]{2,1,0:T(8,128)(2,1)} %maximum_bitcast_fusion), calls=%async_computation.1 | async-start | bytes 22020096 | tf_op jit(solution)/shard_map/all_to_all | solution.py:83
  585.9 306.1 %reduce-scatter.4.cloned.1.call-start = ((), (), s32[]{:S(2)}) async-start(), calls=%async_computation.3 | async-start | bytes 1146880
Sparse Core Ops, SparseCore 0:
  857.6 34.3 reduce-scatter.3
where the time goes:
time: 903 us; the launch traced here: 901 us
  waiting for transfers between devices  622 us (69%)
  starting transfers between devices  151 us (17%)
  local copies, waits for them, and re-layouts  42.7 us (5%)
  matrix products  37.5 us (4%)
  other arithmetic  22.7 us (3%)
  between operations  14.3 us (2%)
  blocking collectives  10.4 us (1%)
    all_to_all x1, waiting for transfers between devices, per_device(): lax.all_to_all(outgoing, 'expert', split_axis=0, concat_axis=0, tiled=True)  347 us
    all_to_all x1, waiting for transfers between devices, per_device(): lax.all_to_all(partials, 'expert', split_axis=0, concat_axis=0, tiled=True)  240 us
    all_to_all x1, starting transfers between devices, per_device(): lax.all_to_all(partials, 'expert', split_axis=0, concat_axis=0, tiled=True)  126 us
    unnamed x2, waiting for transfers between devices  34.6 us
    dot_general x3, matrix products, expert_block(): jnp.dot(hidden, down_piece, preferred_element_type=jnp.float32)  26.8 us
    gather x1, local copies, waits for them, and re-layouts, per_device(): picked = returned[lookup].astype(jnp.float32) * weights_kept[:, None]  19.3 us
  transfers between devices with their start and end apart: 6, of which 3 were waited for; matrix products, arithmetic and copies ran while one was open for 4% of the time, Pallas kernels for 0%

commit v1 on v0

v1 whole, which is shorter than its diff:
```python
import jax
import jax.numpy as jnp
from jax import lax
from jax.sharding import PartitionSpec as P

CAP = 8


def per_device(tokens, expert_ids, gate_weights, replica_plan, w_gate, w_up, w_down):
    owners = lax.axis_size("expert")
    me = lax.axis_index("expert")
    owned = w_gate.shape[0]
    experts = owned * owners
    rows = (owned + 1) * CAP
    tok, feat = tokens.shape
    width = w_gate.shape[1]
    expert_range = jnp.arange(experts, dtype=jnp.int32)
    hit = expert_ids[:, :, None] == expert_range[None, None, :]
    member = jnp.any(hit, axis=1)
    gate = jnp.sum(jnp.where(hit, gate_weights[:, :, None], 0.0), axis=1)
    earlier = jnp.tri(tok, tok, -1, dtype=jnp.bfloat16)
    rank = jnp.dot(earlier, member.astype(jnp.bfloat16), preferred_element_type=jnp.float32)
    key = jnp.where(member, rank.astype(jnp.int32), -1).reshape(tok, owners, owned)
    gate = gate.reshape(tok, owners, owned)
    owner_range = jnp.arange(owners, dtype=jnp.int32)
    planned = jnp.roll(replica_plan, owners // 2) - owner_range * owned
    second = (planned == 1)[None, :]
    key3 = jnp.stack([key[..., 0], key[..., 1], jnp.where(second, key[..., 1], key[..., 0]) - CAP], 2)
    gate3 = jnp.stack([gate[..., 0], gate[..., 1], jnp.where(second, gate[..., 1], gate[..., 0])], 2)
    place = jnp.arange(CAP, dtype=jnp.int32)
    chosen = key3[..., None] == place
    select = chosen.astype(jnp.bfloat16).reshape(tok, owners * rows)
    mix = jnp.where(chosen, gate3[..., None], 0.0).reshape(tok, owners * rows)
    outgoing = lax.dot_general(
        select, tokens, (((0,), (0,)), ((), ())), preferred_element_type=jnp.bfloat16
    ).reshape(owners, rows, feat)
    arrived = lax.all_to_all(outgoing, "expert", split_axis=0, concat_axis=0, tiled=True)
    full = lax.all_gather(arrived.reshape(owners * rows, feat), "dp", axis=0, tiled=False)
    n_dp = full.shape[0]
    full = full.transpose(1, 0, 2).reshape(owners, owned + 1, CAP, width)
    mine = planned[me]
    outs = []
    for slot in range(owned + 1):
        x = full[:, slot].reshape(owners * CAP, width)
        pick = slot if slot < owned else mine
        wg = lax.dynamic_index_in_dim(w_gate, pick, 0, keepdims=False)
        wu = lax.dynamic_index_in_dim(w_up, pick, 0, keepdims=False)
        wd = lax.dynamic_index_in_dim(w_down, pick, 0, keepdims=False)
        g = jnp.dot(x, wg, preferred_element_type=jnp.float32)
        u = jnp.dot(x, wu, preferred_element_type=jnp.float32)
        h = (jax.nn.silu(g) * u).astype(jnp.bfloat16)
        o = jnp.dot(h, wd, preferred_element_type=jnp.float32).astype(jnp.bfloat16)
        outs.append(o.reshape(owners, CAP, width))
    partial = jnp.stack(outs, axis=1).reshape(owners * rows, n_dp, feat).transpose(1, 0, 2)
    summed = lax.psum_scatter(partial, "dp", scatter_dimension=0, tiled=False)
    back = lax.all_to_all(
        summed.reshape(owners, rows, feat), "expert", split_axis=0, concat_axis=0, tiled=True
    ).reshape(owners * rows, feat)
    high = mix.astype(jnp.bfloat16)
    low = (mix - high.astype(jnp.float32)).astype(jnp.bfloat16)
    out = jnp.dot(high, back, preferred_element_type=jnp.float32)
    out = out + jnp.dot(low, back, preferred_element_type=jnp.float32)
    return out.astype(jnp.bfloat16)


def solution(mesh):
    in_specs = (
        P("expert", "dp"),
        P("expert", None),
        P("expert", None),
        P(),
        P("expert", None, "dp"),
        P("expert", None, "dp"),
        P("expert", "dp", None),
    )
    return jax.shard_map(
        per_device, mesh=mesh, in_specs=in_specs, out_specs=P("expert", "dp"), check_vma=False
    )
```

time: 903 us -> 471 us (0.52)
  waiting for transfers between devices: 622 us -> 235 us
  starting transfers between devices: 151 us -> 11.7 us
  blocking collectives: 10.4 us -> 78 us
  local copies, waits for them, and re-layouts: 42.7 us -> 75.8 us
  other arithmetic: 22.7 us -> 12.5 us
    all_to_all x2 -> x1, waiting for transfers between devices: 587 us -> 62.5 us  [per_device(): lax.all_to_all(summed.reshape(owners, rows, feat), 'expert', split_axis=0...]
    all_to_all x2 -> x1, starting transfers between devices: 139 us -> 11.7 us  [per_device(): lax.all_to_all(summed.reshape(owners, rows, feat), 'expert', split_axis=0...]
    reduce_scatter x0 -> x1, waiting for transfers between devices: none -> 99.3 us  [per_device(): summed = lax.psum_scatter(partial, 'dp', scatter_dimension=0, tiled=False)]
    all_to_all x0 -> x1, blocking collectives: none -> 78 us  [per_device(): lax.all_to_all(outgoing, 'expert', split_axis=0, concat_axis=0, tiled=True)]
    all_gather x0 -> x1, waiting for transfers between devices: none -> 73.2 us  [per_device(): lax.all_gather(arrived.reshape(owners * rows, feat), 'dp', axis=0, tiled=...]
    reshape x1 -> x2, local copies, waits for them, and re-layouts: 0.1 us -> 36.8 us  [the longest x1 18.9 us: per_device(): jnp.stack(outs, axis=1).reshape(owners * rows, n_dp, feat)]
    transpose x0 -> x2, local copies, waits for them, and re-layouts: none -> 36.4 us  [the longest x1 25.5 us: per_device(): full = full.transpose(1, 0, 2).reshape(owners, owned + 1, CAP, width)]
    unnamed x2, waiting for transfers between devices: 34.6 us -> 0.03 us
  transfers between devices with their start and end apart: 6 -> 3, of which waited for: 3 -> 3; matrix products, arithmetic and copies ran while one was open for 4% -> 0% of each run, Pallas kernels for 0% -> 0%
where the time goes in v1:
time: 471 us; the launch traced here: 470 us
  waiting for transfers between devices  235 us (50%)
  blocking collectives  78 us (17%)
  local copies, waits for them, and re-layouts  75.8 us (16%)
  matrix products  41 us (9%)
  between operations  15.5 us (3%)
  other arithmetic  12.5 us (3%)
  starting transfers between devices  11.7 us (2%)
    reduce_scatter x1, waiting for transfers between devices, per_device(): summed = lax.psum_scatter(partial, 'dp', scatter_dimension=0, tiled=False)  99.3 us
    all_to_all x1, blocking collectives, per_device(): lax.all_to_all(outgoing, 'expert', split_axis=0, concat_axis=0, tiled=True)  78 us
    all_gather x1, waiting for transfers between devices, per_device(): lax.all_gather(arrived.reshape(owners * rows, feat), 'dp', axis=0, tiled=...  73.2 us
    all_to_all x1, waiting for transfers between devices, per_device(): lax.all_to_all(summed.reshape(owners, rows, feat), 'expert', split_axis=0...  62.5 us
    dot_general x3, matrix products, per_device(): o = jnp.dot(h, wd, preferred_element_type=jnp.float32).astype(jnp.bfloat16)  26.8 us
    transpose x1, local copies, waits for them, and re-layouts, per_device(): full = full.transpose(1, 0, 2).reshape(owners, owned + 1, CAP, width)  25.5 us
    reshape x1, local copies, waits for them, and re-layouts, per_device(): jnp.stack(outs, axis=1).reshape(owners * rows, n_dp, feat)  18.9 us
    reshape x1, local copies, waits for them, and re-layouts, per_device(): full = full.transpose(1, 0, 2).reshape(owners, owned + 1, CAP, width)  17.9 us
  transfers between devices with their start and end apart: 3, of which 3 were waited for; matrix products, arithmetic and copies ran while one was open for 0% of the time, Pallas kernels for 0%

profile of v1, /device:TPU:2, one launch (start us, length us, event | category | flops | bytes accessed | tf_op | source)
XLA Modules:
  0.0 469.6 jit_solution(9365156542345243629)
XLA Ops:
  6.5 0.0 copy-start
  6.5 0.0 all-gather.2.cloned.1.call-start
  6.5 0.8 fusion.83
  7.3 0.8 copy.35
  8.1 0.3 fusion.69
  8.4 0.1 copy.36
  8.5 0.1 broadcast_compare_fusion
  8.6 0.2 fusion.46
  8.8 0.1 fusion.76
  9.0 0.1 pad_add_fusion
  9.1 0.1 eq.72
  9.2 0.3 bitcast_compare_fusion
  9.5 0.0 copy-done
  9.5 0.9 fusion.73
  10.4 78.0 %all_to_all.10 = bf16[64,24,896]{2,1,0:T(8,128)(2,1)} all-to-all(bf16[64,24,896]{2,1,0:T(8,128)(2,1)S(1)} %fusion.73), channel_id=1, replica_groups=mesh['expert'=64,'dp'=4] {'expert'}, dimensions={0} | all-to-all | bytes 5505024 | tf_op jit(solution)/shard_map/all_to_all | solution.py:37
  88.3 0.0 all-gather.2.cloned.1.call-update
  88.4 0.0 reduce-scatter.2.cloned.1.call-start
  88.4 0.6 dynamic_slice.40
  90.9 73.2 %all-gather.2.cloned.1.call-done = bf16[4,1536,896]{2,1,0:T(8,128)(2,1)} async-done(((bf16[1,1536,896]{2,1,0:T(8,128)(2,1)}), bf16[4,1536,896]{2,1,0:T(8,128)(2,1)}) %all-gather.2.cloned.1.call-update) | async-done | bytes 11010064 | tf_op jit(solution)/shard_map/all_gather | solution.py:38
  164.1 25.5 %copy.39 = bf16[1536,4,896]{2,1,0:T(4,128)(2,1)} copy(bf16[1536,4,896]{2,0,1:T(8,128)(2,1)} %bitcast.116) | data formatting | bytes 22020096 | tf_op jit(solution)/shard_map/transpose | solution.py:40
  189.6 17.9 %reshape.130 = bf16[64,3,8,3584]{3,2,1,0:T(8,128)(2,1)} reshape(bf16[1536,4,896]{2,1,0:T(4,128)(2,1)} %copy.39) | data formatting | bytes 22020096 | tf_op jit(solution)/shard_map/reshape | solution.py:40
  207.6 0.0 copy-start.3
  207.6 3.9 fusion.4
  211.4 0.0 copy-done.3
  211.4 3.1 fusion.6
  214.6 3.2 fusion.8
  217.8 9.0 %fusion.2 = bf16[64,1,8,3584]{3,2,1,0:T(8,128)(2,1)} fusion(bf16[2,256,3584]{2,1,0:T(8,128)(2,1)} %param.13, s32[]{:T(128)S(6)} %select_n.61, bf16[2,3584,256]{2,1,0:T(8,128)(2,1)} %param.12, bf16[64,3,8,3584]{3,2,1,0:T(8,128)(2,1)} %reshape.130, f32[512,256]{1,0:T(8,128)S(1)} %fusion.8), kind=kOutput, calls=%fused_computation.6 | convolution fusion | flops 1881669632 | bytes 11535360 | tf_op jit(solution)/shard_map/dot_general | solution.py:52
  226.8 8.9 %fusion = bf16[64,1,8,3584]{3,2,1,0:T(8,128)(2,1)} fusion(bf16[2,256,3584]{2,1,0:T(8,128)(2,1)} %param.13, bf16[2,3584,256]{2,1,0:T(8,128)(2,1)} %param.12, bf16[64,3,8,3584]{3,2,1,0:T(8,128)(2,1)} %reshape.130, f32[512,256]{1,0:T(8,128)S(1)} %fusion.4), kind=kOutput, calls=%fused_computation.4 | convolution fusion | flops 1881669632 | bytes 11534336 | tf_op jit(solution)/shard_map/dot_general | solution.py:52
  235.6 8.9 %fusion.1 = bf16[64,1,8,3584]{3,2,1,0:T(8,128)(2,1)} fusion(bf16[2,256,3584]{2,1,0:T(8,128)(2,1)} %param.13, bf16[2,3584,256]{2,1,0:T(8,128)(2,1)} %param.12, bf16[64,3,8,3584]{3,2,1,0:T(8,128)(2,1)} %reshape.130, f32[512,256]{1,0:T(8,128)S(1)} %fusion.6), kind=kOutput, calls=%fused_computation.5 | convolution fusion | flops 1881669632 | bytes 11534336 | tf_op jit(solution)/shard_map/dot_general | solution.py:52
  244.5 10.2 %pad_maximum_fusion = bf16[64,3,8,3584]{3,2,1,0:T(8,128)(2,1)} fusion(bf16[64,1,8,3584]{3,2,1,0:T(8,128)(2,1)} %fusion.2, bf16[64,1,8,3584]{3,2,1,0:T(8,128)(2,1)} %fusion.1, bf16[64,1,8,3584]{3,2,1,0:T(8,128)(2,1)} %fusion), kind=kLoop, calls=%fused_computation | loop fusion | flops 11010048 | bytes 22020096 | tf_op jit(solution)/shard_map/stack | solution.py:54
  254.7 18.9 %reshape.131 = bf16[1536,4,896]{2,1,0:T(4,128)(2,1)} reshape(bf16[64,3,8,3584]{3,2,1,0:T(8,128)(2,1)} %pad_maximum_fusion) | data formatting | bytes 22020096 | tf_op jit(solution)/shard_map/reshape | solution.py:54
  273.6 10.9 %copy.43 = bf16[4,1536,896]{2,1,0:T(8,128)(2,1)} copy(bf16[4,1536,896]{2,0,1:T(4,128)(2,1)} %bitcast.113) | data formatting | bytes 22020096 | tf_op jit(solution)/shard_map/transpose | solution.py:54
  284.4 0.0 reduce-scatter.2.cloned.1.call-update
  284.5 0.0 copy-start.2
  284.5 99.3 %reduce-scatter.2.cloned.1.call-done = bf16[1,1536,896]{2,1,0:T(8,128)(2,1)} async-done(((bf16[4,1536,896]{2,1,0:T(8,128)(2,1)}), bf16[1,1536,896]{2,1,0:T(8,128)(2,1)}) %reduce-scatter.2.cloned.1.call-update) | async-done | bytes 2752528 | tf_op jit(solution)/shard_map/reduce_scatter | solution.py:55
  383.8 11.7 %all-to-all-start.1 = ((bf16[64,24,896]{2,1,0:T(8,128)(2,1)}), bf16[64,24,896]{2,1,0:T(8,128)(2,1)S(1)}, u32[]{:S(2)}, u32[]{:S(2)}) async-start(bf16[64,24,896]{2,1,0:T(8,128)(2,1)} %bitcast.118), calls=%async_computation.2 | async-start | bytes 5505024 | tf_op jit(solution)/shard_map/all_to_all | solution.py:56
  395.5 0.0 copy-done.2
  395.5 0.1 copy.37
  395.6 0.3 select_reduce_fusion
  395.9 0.1 copy.38
  396.0 0.1 broadcast_select_fusion
  396.2 0.1 pad_maximum_fusion.1
  396.3 0.9 select_convert_fusion
  397.1 0.1 fusion.47
  397.3 62.5 %all-to-all-done.1 = bf16[64,24,896]{2,1,0:T(8,128)(2,1)S(1)} async-done(((bf16[64,24,896]{2,1,0:T(8,128)(2,1)}), bf16[64,24,896]{2,1,0:T(8,128)(2,1)S(1)}, u32[]{:S(2)}, u32[]{:S(2)}) %all-to-all-start.1) | async-done | bytes 2752544 | tf_op jit(solution)/shard_map/all_to_all | solution.py:56
  459.8 0.0 copy-start.1
  459.8 1.6 fusion.84
  461.4 1.3 fusion.45
  462.7 0.0 copy-done.1
  (2 shorter events, 0.0 us)
Async XLA Ops:
  6.5 3.0 copy-start
  6.5 157.6 %all-gather.2.cloned.1.call-start = ((), (), s32[]{:S(2)}) async-start(), calls=%async_computation.3 | async-start | bytes 13762560 | tf_op jit(solution)/shard_map/all_gather | solution.py:38
  88.4 295.4 %reduce-scatter.2.cloned.1.call-start = ((), (), s32[]{:S(2)}) async-start(), calls=%async_computation.4 | async-start | bytes 13762560 | tf_op jit(solution)/shard_map/reduce_scatter | solution.py:55
  207.6 3.9 copy-start.3
  284.5 111.0 %copy-start.2 = (f32[128,8]{0,1:T(8,128)S(1)}, f32[128,8]{0,1:T(8,128)}, u32[]{:S(2)}) copy-start(f32[128,8]{0,1:T(8,128)} %param.9) | copy-start | bytes 12292
  383.8 76.0 %all-to-all-start.1 = ((bf16[64,24,896]{2,1,0:T(8,128)(2,1)}), bf16[64,24,896]{2,1,0:T(8,128)(2,1)S(1)}, u32[]{:S(2)}, u32[]{:S(2)}) async-start(bf16[64,24,896]{2,1,0:T(8,128)(2,1)} %bitcast.118), calls=%async_computation.2 | async-start | bytes 5505024 | tf_op jit(solution)/shard_map/all_to_all | solution.py:56
  459.8 3.0 copy-start.1
Sparse Core Ops, SparseCore 0:
  88.5 75.6 all-gather.1
  284.6 99.1 reduce-scatter.1

commit v2 on v1

v2 whole, which is shorter than its diff:
```python
import functools

import jax
import jax.numpy as jnp
from jax import lax
from jax.experimental import pallas as pl
from jax.experimental.pallas import tpu as pltpu
from jax.sharding import PartitionSpec as P

CAP = 8
N_LO, N_Y, N_HI, N_CORE = 2, 4, 2, 2
N_X = N_LO * N_HI
GROUPS = 3
ROWS = GROUPS * 2 * CAP
CHUNKS = ((0, 1), (-2, 3), (-3, 4), (-1, 2))
BF16, F32 = jnp.bfloat16, jnp.float32


def kernel(
    n_z, tok_ref, meta_ref, plan_ref, wg_hbm, wu_hbm, wd_hbm, out_ref,
    wg, wu, wd, toks, metas, picks, mix_hi, mix_lo, g_buf, y_in, x_buf, relay, core_in,
    x_back, relay_back, y_out, y_back, z_out, z_back,
    send_sem, recv_sem, local_sem,
):
    expert = lax.axis_index("expert")
    dp = lax.axis_index("dp")
    z, lo, y = expert // (N_LO * N_Y), (expert // N_Y) % N_LO, expert % N_Y
    hi, core = dp // N_CORE, dp % N_CORE
    x = hi * N_LO + lo
    n_tok = tok_ref.shape[0]
    feat = tok_ref.shape[1]
    hidden = wg.shape[2]
    n_chunk = len(CHUNKS)

    def device(z_, x_, y_, core_):
        return ((z_ * N_LO + x_ % N_LO) * N_Y + y_, (x_ // N_LO) * N_CORE + core_)

    def along_z(step):
        return device((z + step + n_z) % n_z, x, y, core)

    def along_y(step):
        return device(z, x, (y + step) % N_Y, core)

    def along_x(step):
        return device(z, (x + step) % N_X, y, core)

    right, left = (x + 1) % N_X, (x + N_X - 1) % N_X
    across = (x + 2) % N_X
    partner = device(z, x, y, 1 - core)

    started = []
    count = [0]
    local_count = [0]

    def remote(src, dst, target):
        i = count[0]
        count[0] += 1
        copy = pltpu.make_async_remote_copy(
            src_ref=src, dst_ref=dst, send_sem=send_sem.at[i], recv_sem=recv_sem.at[i],
            device_id=target, device_id_type=pl.DeviceIdType.MESH,
        )
        copy.start()
        started.append(copy)
        return copy

    def local(src, dst):
        i = local_count[0]
        local_count[0] += 1
        copy = pltpu.make_async_copy(src, dst, local_sem.at[i])
        copy.start()
        return copy

    def received(copies):
        for c in copies:
            c.wait_recv()

    def sent(copies):
        for c in copies:
            c.wait_send()
            started[:] = [other for other in started if other is not c]

    weight_loads = [
        local(wg_hbm, wg.at[pl.ds(0, 2)]),
        local(wu_hbm, wu.at[pl.ds(0, 2)]),
        local(wd_hbm, wd.at[pl.ds(0, 2)]),
    ]
    where = {d: (c, j) for c, pair in enumerate(CHUNKS) for j, d in enumerate(pair)}
    own_loads = [local(tok_ref, toks.at[where[0]]), local(meta_ref, metas.at[where[0]])]

    barrier = pltpu.get_barrier_semaphore()
    peers = [along_z(s) for s in range(1, n_z)] + [along_y(s) for s in range(1, N_Y)]
    peers += [along_x(1), along_x(3), partner]
    for peer in peers:
        pl.semaphore_signal(barrier, inc=1, device_id=peer, device_id_type=pl.DeviceIdType.MESH)
    pl.semaphore_wait(barrier, len(peers))

    z_in = {}

    def z_forward(d):
        step = 1 if d > 0 else -1
        for s in ((step,) if d else (1, -1)):
            if d:
                received(z_in[d])
                src_t, src_m = toks.at[where[d]], metas.at[where[d]]
            else:
                src_t, src_m = tok_ref, meta_ref
            nxt = d + s
            if nxt in where:
                z_in[nxt] = [
                    remote(src_t, toks.at[where[nxt]], along_z(-s)),
                    remote(src_m, metas.at[where[nxt]], along_z(-s)),
                ]

    before = (
        lax.broadcasted_iota(jnp.int32, (n_tok, n_tok), 0)
        < lax.broadcasted_iota(jnp.int32, (n_tok, n_tok), 1)
    ).astype(F32).astype(BF16)
    plane = N_LO * N_Y
    place = lax.broadcasted_iota(jnp.int32, (CAP, n_tok), 0).astype(F32)
    blank = jnp.zeros((CAP, n_tok), F32)

    def planned_of(owner):
        owners = n_z * plane
        return (plan_ref[(owner + owners // 2) % owners] - 2 * owner).astype(F32)

    def slots(c):
        keys, gates = [], []
        ids = lax.broadcasted_iota(jnp.int32, (2 * plane, n_tok), 0) + z * (2 * plane)
        ids = ids.astype(F32)
        for j in range(2):
            meta = metas[c, j]
            member = jnp.zeros((2 * plane, n_tok), F32)
            gate = jnp.zeros((2 * plane, n_tok), F32)
            for k in range(8):
                hit = meta[k : k + 1, :] == ids
                member = jnp.where(hit, 1.0, member)
                gate = jnp.where(hit, meta[8 + k : 9 + k, :], gate)
            rank = jnp.dot(member.astype(BF16), before, preferred_element_type=F32)
            keys.append(jnp.where(member > 0.5, rank, -1.0))
            gates.append(gate)
        for yy in range(N_Y):
            for ll in range(N_LO):
                r = ll * (2 * N_Y) + yy * 2
                f = planned_of(z * plane + ll * N_Y + yy)
                base = (yy * N_LO + ll) * ROWS
                for g in range(GROUPS):
                    ones, weights = [], []
                    for j in range(2):
                        k0, k1 = keys[j][r : r + 1, :], keys[j][r + 1 : r + 2, :]
                        w0, w1 = gates[j][r : r + 1, :], gates[j][r + 1 : r + 2, :]
                        if g == 0:
                            k, w = k0, w0
                        elif g == 1:
                            k, w = k1, w1
                        else:
                            k = k0 * (1.0 - f) + k1 * f - float(CAP)
                            w = w0 * (1.0 - f) + w1 * f
                        hit = jnp.broadcast_to(k, (CAP, n_tok)) == place
                        one = jnp.where(hit, 1.0, 0.0)
                        weight = jnp.where(hit, jnp.broadcast_to(w, (CAP, n_tok)), 0.0)
                        row1 = [blank, blank]
                        row2 = [blank, blank]
                        row1[j], row2[j] = one, weight
                        ones.append(jnp.concatenate(row1, axis=1))
                        weights.append(jnp.concatenate(row2, axis=1))
                    at = pl.ds(base + g * 2 * CAP, 2 * CAP)
                    picks[at, :] = jnp.concatenate(ones, axis=0).astype(BF16)
                    w = jnp.concatenate(weights, axis=0)
                    high = w.astype(BF16)
                    mix_hi[c, at, :] = high
                    mix_lo[c, at, :] = (w - high.astype(F32)).astype(BF16)

    y_moves, x_moves, x_relays, x_fwd, core_moves, own_moves = {}, {}, {}, {}, {}, {}
    reduce_moves, b_moves, b_relays, b_fwd, yb_moves, zb_moves = {}, {}, {}, {}, {}, {}

    def d1(c):
        slots(c)
        both = toks[c].reshape(2 * n_tok, feat)
        rows = jnp.dot(picks[...], both, preferred_element_type=F32).astype(BF16)
        g_buf[c] = rows.reshape(N_Y, N_LO, ROWS, feat)
        y_moves[c] = [
            remote(g_buf.at[c, (y + s) % N_Y], y_in.at[c, :, y], along_y(s)) for s in (2, 1, 3)
        ]
        own_moves[c] = local(g_buf.at[c, y], y_in.at[c, :, y])

    half = N_Y // 2

    def d2(c):
        own_moves[c].wait()
        received(y_moves[c])
        mine = y_in.at[c, lo]
        x_relays[c] = [
            remote(mine.at[pl.ds(0, half)], relay.at[c, 0], along_x(1)),
            remote(mine.at[pl.ds(half, half)], relay.at[c, 1], along_x(3)),
        ]
        x_moves[c] = [
            remote(y_in.at[c, 1 - lo], x_buf.at[c, hi, core, lo], along_x(1)),
            remote(y_in.at[c, 1 - lo], x_buf.at[c, hi, core, lo], along_x(3)),
        ]
        core_moves[c] = [remote(mine, x_buf.at[c, hi, core, lo], partner)]
        own_moves[c] = local(mine, x_buf.at[c, hi, core, lo])

    def d3(c):
        received(x_relays[c])
        x_fwd[c] = [
            remote(relay.at[c, 0], x_buf.at[c, left // N_LO, core, 1 - lo, pl.ds(0, half)], along_x(1)),
            remote(relay.at[c, 1], x_buf.at[c, right // N_LO, core, 1 - lo, pl.ds(half, half)], along_x(3)),
        ]

    def d4(c):
        received(x_moves[c])
        for other in (left, right):
            block = x_buf.at[c, other // N_LO, core, 1 - lo]
            core_moves[c].append(remote(block, block, partner))
        received(x_fwd[c])
        block = x_buf.at[c, across // N_LO, core, lo]
        core_moves[c].append(remote(block, block, partner))

    def d5(c):
        own_moves[c].wait()
        received(core_moves[c])
        sent(core_moves[c])

        def group(g, carry):
            at = pl.ds(pl.multiple_of(g * 2 * CAP, 2 * CAP), 2 * CAP)
            m = N_LO * N_Y * 2 * CAP
            gate = jnp.zeros((m, hidden), F32)
            up = jnp.zeros((m, hidden), F32)
            for q in range(4):
                rows = x_buf[c, q // 2, q % 2, :, :, at, :].reshape(m, feat)
                ks = pl.ds(q * feat, feat)
                gate += jnp.dot(rows, wg[g, ks, :], preferred_element_type=F32)
                up += jnp.dot(rows, wu[g, ks, :], preferred_element_type=F32)
            h = (gate / (1.0 + jnp.exp(-gate)) * up).astype(BF16)
            for q in range(4):
                o = jnp.dot(h, wd[g, :, pl.ds(q * feat, feat)], preferred_element_type=F32)
                x_buf[c, q // 2, q % 2, :, :, at, :] = o.astype(BF16).reshape(
                    N_LO, N_Y, 2 * CAP, feat
                )
            return carry

        lax.fori_loop(0, GROUPS, group, 0)
        reduce_moves[c] = remote(x_buf.at[c, :, 1 - core], core_in.at[c], partner)

    def r1(c):
        received([reduce_moves[c]])

        def add(i, carry):
            h_, s_, y_ = i // (N_LO * N_Y), (i // N_Y) % N_LO, i % N_Y
            total = x_buf[c, h_, core, s_, y_].astype(F32) + core_in[c, h_, s_, y_].astype(F32)
            x_buf[c, h_, core, s_, y_] = total.astype(BF16)
            return carry

        lax.fori_loop(0, N_HI * N_LO * N_Y, add, 0)
        far = x_buf.at[c, across // N_LO, core, lo]
        b_relays[c] = [
            remote(far.at[pl.ds(0, half)], relay_back.at[c, 0], along_x(1)),
            remote(far.at[pl.ds(half, half)], relay_back.at[c, 1], along_x(3)),
        ]
        b_moves[c] = [
            remote(x_buf.at[c, right // N_LO, core, 1 - lo], x_back.at[c, 0], along_x(1)),
            remote(x_buf.at[c, left // N_LO, core, 1 - lo], x_back.at[c, 1], along_x(3)),
        ]

    def r2(c):
        received(b_relays[c])
        b_fwd[c] = [
            remote(relay_back.at[c, 0], x_back.at[c, 2, pl.ds(0, half)], along_x(1)),
            remote(relay_back.at[c, 1], x_back.at[c, 2, pl.ds(half, half)], along_x(3)),
        ]

    def r3(c):
        received(b_moves[c])
        received(b_fwd[c])

        def add(i, carry):
            y_out[c, 1 - lo, i] = (x_back[c, 0, i].astype(F32) + x_back[c, 1, i].astype(F32)).astype(BF16)
            y_out[c, lo, i] = (x_buf[c, hi, core, lo, i].astype(F32) + x_back[c, 2, i].astype(F32)).astype(BF16)
            return carry

        lax.fori_loop(0, N_Y, add, 0)
        yb_moves[c] = [
            remote(y_out.at[c, :, (y + s) % N_Y], y_back.at[c, y], along_y(s)) for s in (2, 1, 3)
        ]
        own_moves[c] = local(y_out.at[c, :, y], y_back.at[c, y])

    def r4(c):
        own_moves[c].wait()
        received(yb_moves[c])
        rows = y_back[c].reshape(N_Y * N_LO * ROWS, feat)
        dims = (((0,), (0,)), ((), ()))
        total = lax.dot_general(mix_hi[c], rows, dims, preferred_element_type=F32)
        total = total + lax.dot_general(mix_lo[c], rows, dims, preferred_element_type=F32)
        z_out[c] = total.astype(BF16).reshape(2, n_tok, feat)
        for j, d in enumerate(CHUNKS[c]):
            if d:
                zb_moves[c, j] = remote(z_out.at[c, j], z_back.at[c, j], along_z(d))
            else:
                own_z.append(local(z_out.at[c, j], z_back.at[c, j]))

    own_z = []

    def load_weights():
        for load in weight_loads:
            load.wait()
        f = planned_of(expert)

        def pick_rows(i, carry):
            at = pl.ds(pl.multiple_of(i * 128, 128), 128)
            for w in (wg, wu):
                w[2, at, :] = (w[0, at, :].astype(F32) * (1.0 - f) + w[1, at, :].astype(F32) * f).astype(BF16)
            return carry

        lax.fori_loop(0, wg.shape[1] // 128, pick_rows, 0)

        def pick_down(i, carry):
            at = pl.ds(pl.multiple_of(i * 16, 16), 16)
            wd[2, at, :] = (wd[0, at, :].astype(F32) * (1.0 - f) + wd[1, at, :].astype(F32) * f).astype(BF16)
            return carry

        lax.fori_loop(0, hidden // 16, pick_down, 0)

    z_forward(0)
    z_forward(1)
    z_forward(-1)
    for load in own_loads:
        load.wait()
    d1(0)
    load_weights()
    z_forward(2)
    z_forward(-2)
    d2(0)
    z_forward(3)
    z_forward(-3)
    d1(1)
    d3(0)
    z_forward(4)
    d1(2)
    d2(1)
    d4(0)
    d1(3)
    d3(1)
    d5(0)
    d2(2)
    d4(1)
    r1(0)
    d3(2)
    d5(1)
    d2(3)
    d4(2)
    r1(1)
    r2(0)
    d3(3)
    d5(2)
    r3(0)
    d4(3)
    r1(2)
    r2(1)
    d5(3)
    r1(3)
    r2(2)
    r3(1)
    r4(0)
    r2(3)
    r3(2)
    r4(1)
    r3(3)
    r4(2)
    r4(3)
    for copy in own_z:
        copy.wait()
    received(zb_moves.values())

    def finish(i, carry):
        at = pl.ds(pl.multiple_of(i * 16, 16), 16)
        total = jnp.zeros((16, feat), F32)
        for c in range(n_chunk):
            for j in range(2):
                total = total + z_back[c, j, at, :].astype(F32)
        out_ref[at, :] = total.astype(out_ref.dtype)
        return carry

    lax.fori_loop(0, n_tok // 16, finish, 0)
    sent(list(started))


N_REMOTE = 14 + 4 * (3 + 6 + 4 + 1 + 6 + 3) + 7
N_LOCAL = 5 + 4 * 3 + 1


def per_device(tokens, expert_ids, gate_weights, replica_plan, w_gate, w_up, w_down):
    owners = lax.axis_size("expert")
    n_z = owners // (N_LO * N_Y)
    tok, feat = tokens.shape
    width = w_gate.shape[1]
    hidden = w_gate.shape[2]
    meta = jnp.concatenate([expert_ids.T.astype(F32), gate_weights.T], axis=0)
    n_chunk = len(CHUNKS)
    vmem = pl.BlockSpec(memory_space=pltpu.VMEM)
    hbm = pl.BlockSpec(memory_space=pl.ANY)
    block = (N_Y, ROWS, feat)
    slot_rows = N_Y * N_LO * ROWS
    return pl.pallas_call(
        functools.partial(kernel, n_z),
        out_shape=jax.ShapeDtypeStruct((tok, feat), BF16),
        in_specs=[vmem, vmem, pl.BlockSpec(memory_space=pltpu.SMEM), hbm, hbm, hbm],
        out_specs=vmem,
        scratch_shapes=[
            pltpu.VMEM((3, width, hidden), BF16),
            pltpu.VMEM((3, width, hidden), BF16),
            pltpu.VMEM((3, hidden, width), BF16),
            pltpu.VMEM((n_chunk, 2, tok, feat), BF16),
            pltpu.VMEM((n_chunk, 2, 16, tok), F32),
            pltpu.VMEM((slot_rows, 2 * tok), BF16),
            pltpu.VMEM((n_chunk, slot_rows, 2 * tok), BF16),
            pltpu.VMEM((n_chunk, slot_rows, 2 * tok), BF16),
            pltpu.VMEM((n_chunk, N_Y, N_LO, ROWS, feat), BF16),
            pltpu.VMEM((n_chunk, N_LO) + block, BF16),
            pltpu.VMEM((n_chunk, N_HI, N_CORE, N_LO) + block, BF16),
            pltpu.VMEM((n_chunk, 2, N_Y // 2, ROWS, feat), BF16),
            pltpu.VMEM((n_chunk, N_HI, N_LO) + block, BF16),
            pltpu.VMEM((n_chunk, 3) + block, BF16),
            pltpu.VMEM((n_chunk, 2, N_Y // 2, ROWS, feat), BF16),
            pltpu.VMEM((n_chunk, N_LO) + block, BF16),
            pltpu.VMEM((n_chunk, N_Y, N_LO, ROWS, feat), BF16),
            pltpu.VMEM((n_chunk, 2, tok, feat), BF16),
            pltpu.VMEM((n_chunk, 2, tok, feat), BF16),
            pltpu.SemaphoreType.DMA((N_REMOTE,)),
            pltpu.SemaphoreType.DMA((N_REMOTE,)),
            pltpu.SemaphoreType.DMA((N_LOCAL,)),
        ],
        compiler_params=pltpu.CompilerParams(
            collective_id=0, has_side_effects=True, vmem_limit_bytes=67043328
        ),
    )(tokens, meta, replica_plan, w_gate, w_up, w_down)


def solution(mesh):
    in_specs = (
        P("expert", "dp"),
        P("expert", None),
        P("expert", None),
        P(),
        P("expert", None, "dp"),
        P("expert", None, "dp"),
        P("expert", "dp", None),
    )
    return jax.shard_map(
        per_device, mesh=mesh, in_specs=in_specs, out_specs=P("expert", "dp"), check_vma=False
    )
```

time: 471 us -> 193 us (0.41)
  waiting for transfers between devices: 235 us -> 0 us
  Pallas kernels: 0 us -> 189 us
  blocking collectives: 78 us -> 0 us
  local copies, waits for them, and re-layouts: 75.8 us -> 1.65 us
  matrix products: 41 us -> 0 us
  between operations: 15.5 us -> 0.01 us
  starting transfers between devices: 11.7 us -> 0 us
  other arithmetic: 12.5 us -> 1.97 us
    pallas_call x0 -> x1, Pallas kernels: none -> 189 us  [per_device(): pl.pallas_call(functools.partial(kernel, n_z), out_shape=jax.ShapeDtypeSt...]
    reduce_scatter x1 -> x0, waiting for transfers between devices: 99.3 us -> none  [per_device(): summed = lax.psum_scatter(partial, 'dp', scatter_dimension=0, tiled=False)]
    all_to_all x1 -> x0, blocking collectives: 78 us -> none  [per_device(): lax.all_to_all(outgoing, 'expert', split_axis=0, concat_axis=0, tiled=True)]
    all_gather x1 -> x0, waiting for transfers between devices: 73.2 us -> none  [per_device(): lax.all_gather(arrived.reshape(owners * rows, feat), 'dp', axis=0, tiled=...]
    all_to_all x1 -> x0, waiting for transfers between devices: 62.5 us -> none  [per_device(): lax.all_to_all(summed.reshape(owners, rows, feat), 'expert', split_axis=0...]
    dot_general x10 -> x0, matrix products: 41 us -> none  [the longest x3 26.8 us: per_device(): o = jnp.dot(h, wd, preferred_element_type=jnp.float32).astype(jnp.bfloat16)]
    reshape x2 -> x0, local copies, waits for them, and re-layouts: 36.8 us -> none  [the longest x1 18.9 us: per_device(): jnp.stack(outs, axis=1).reshape(owners * rows, n_dp, feat)]
    transpose x2 -> x0, local copies, waits for them, and re-layouts: 36.4 us -> none  [the longest x1 25.5 us: per_device(): full = full.transpose(1, 0, 2).reshape(owners, owned + 1, CAP, width)]
  transfers between devices with their start and end apart: 3 -> 0, of which waited for: 3 -> 0; matrix products, arithmetic and copies ran while one was open for 0% -> 0% of each run, Pallas kernels for 0% -> 0%
where the time goes in v2:
time: 193 us
  Pallas kernels  189 us (98%)
  other arithmetic  1.97 us (1%)
    pallas_call x1, Pallas kernels, per_device(): pl.pallas_call(functools.partial(kernel, n_z), out_shape=jax.ShapeDtypeSt...  189 us

profile of v2, /device:TPU:2, one launch (start us, length us, event | category | flops | bytes accessed | tf_op | source)
XLA Modules:
  0.0 192.6 jit_solution(6401771270302233158)
XLA Ops:
  0.0 0.7 convert_bitcast_fusion
  0.7 1.3 pad_maximum_fusion.meta_ref
  2.0 189.0 %shard_map.73 = bf16[128,896]{1,0:T(8,128)(2,1)} custom-call(bf16[128,896]{1,0:T(8,128)(2,1)} %tok_ref.1, f32[16,128]{1,0:T(8,128)} %pad_maximum_fusion.meta_ref, s32[64]{0:T(128)} %plan_ref.1, bf16[2,3584,256]{2,1,0:T(8,128)(2,1)} %wg_hbm.1, bf16[2,3584,256]{2,1,0:T(8,128)(2,1)} %wu_hbm.1, bf16[2,256,3584]{2,1,0:T(8,128)(2,1)} %wd_hbm.1), custom_call_target="tpu_custom_call" | custom-call | tf_op jit(solution)/shard_map/pallas_call | solution.py:403
  191.0 1.6 copy.9

commit v3 on v2

--- a/solution.py
+++ b/solution.py
@@ -12,14 +12,15 @@
 N_X = N_LO * N_HI
 GROUPS = 3
 ROWS = GROUPS * 2 * CAP
-CHUNKS = ((0, 1), (-2, 3), (-3, 4), (-1, 2))
+CHUNKS = ((1, -1), (2, -2), (3, -3), (0, 4))
+PIECES = (1, 1, 1, 2)
 BF16, F32 = jnp.bfloat16, jnp.float32
 
 
 def kernel(
-    n_z, tok_ref, meta_ref, plan_ref, wg_hbm, wu_hbm, wd_hbm, out_ref,
-    wg, wu, wd, toks, metas, picks, mix_hi, mix_lo, g_buf, y_in, x_buf, relay, core_in,
-    x_back, relay_back, y_out, y_back, z_out, z_back,
+    n_z, tok_ref, ids_ref, gate_ref, plan_ref, wg_hbm, wu_hbm, wd_hbm, out_ref,
+    wg, wu, wd, toks, metas, meta_own, picks, mix_hi, mix_lo, g_buf, g_far, y_in, x_buf, core_in,
+    x_back, y_out, y_back, z_out, z_back,
     send_sem, recv_sem, local_sem,
 ):
     expert = lax.axis_index("expert")
@@ -85,31 +86,45 @@
         local(wd_hbm, wd.at[pl.ds(0, 2)]),
     ]
     where = {d: (c, j) for c, pair in enumerate(CHUNKS) for j, d in enumerate(pair)}
-    own_loads = [local(tok_ref, toks.at[where[0]]), local(meta_ref, metas.at[where[0]])]
+
+    def tok_at(d, h):
+        c, j = where[d]
+        return toks.at[c, h, j]
+
+    own_loads = [local(tok_ref, tok_at(0, hi))]
+    meta_own[pl.ds(0, 8), :] = ids_ref[...].astype(F32)
+    meta_own[pl.ds(8, 8), :] = gate_ref[...]
+    metas[where[0]] = meta_own[...]
 
     barrier = pltpu.get_barrier_semaphore()
     peers = [along_z(s) for s in range(1, n_z)] + [along_y(s) for s in range(1, N_Y)]
-    peers += [along_x(1), along_x(3), partner]
+    peers += [along_x(1), along_x(2), along_x(3), partner]
     for peer in peers:
         pl.semaphore_signal(barrier, inc=1, device_id=peer, device_id_type=pl.DeviceIdType.MESH)
     pl.semaphore_wait(barrier, len(peers))
 
-    z_in = {}
-
-    def z_forward(d):
-        step = 1 if d > 0 else -1
-        for s in ((step,) if d else (1, -1)):
+    z_in, z_meta = {}, {}
+
+    def z_near(d):
+        for s in ((1, -1) if d == 0 else (1,) if d > 0 else (-1,)):
             if d:
-                received(z_in[d])
-                src_t, src_m = toks.at[where[d]], metas.at[where[d]]
-            else:
-                src_t, src_m = tok_ref, meta_ref
+                received([z_in[d, 0], z_meta[d]])
             nxt = d + s
             if nxt in where:
-                z_in[nxt] = [
-                    remote(src_t, toks.at[where[nxt]], along_z(-s)),
-                    remote(src_m, metas.at[where[nxt]], along_z(-s)),
-                ]
+                src = tok_at(d, hi) if d else tok_ref
+                src_m = metas.at[where[d]] if d else meta_own
+                z_in[nxt, 0] = remote(src, tok_at(nxt, hi), along_z(-s))
+                z_meta[nxt] = remote(src_m, metas.at[where[nxt]], along_z(-s))
+
+    def z_far(d):
+        received([z_in[d, 1]])
+        for s in ((1, -1) if d == 0 else (1,) if d > 0 else (-1,)):
+            nxt = d + s
+            if nxt in where:
+                z_in[nxt, 1] = remote(tok_at(d, 1 - hi), tok_at(nxt, 1 - hi), along_z(-s))
+
+    def swap():
+        z_in[0, 1] = remote(tok_ref, tok_at(0, hi), along_x(2))
 
     before = (
         lax.broadcasted_iota(jnp.int32, (n_tok, n_tok), 0)
@@ -142,7 +157,7 @@
             for ll in range(N_LO):
                 r = ll * (2 * N_Y) + yy * 2
                 f = planned_of(z * plane + ll * N_Y + yy)
-                base = (yy * N_LO + ll) * ROWS
+                base = (ll * N_Y + yy) * ROWS
                 for g in range(GROUPS):
                     ones, weights = [], []
                     for j in range(2):
@@ -164,60 +179,61 @@
                         ones.append(jnp.concatenate(row1, axis=1))
                         weights.append(jnp.concatenate(row2, axis=1))
                     at = pl.ds(base + g * 2 * CAP, 2 * CAP)
-                    picks[at, :] = jnp.concatenate(ones, axis=0).astype(BF16)
+                    picks[c, at, :] = jnp.concatenate(ones, axis=0).astype(BF16)
                     w = jnp.concatenate(weights, axis=0)
                     high = w.astype(BF16)
                     mix_hi[c, at, :] = high
                     mix_lo[c, at, :] = (w - high.astype(F32)).astype(BF16)
 
-    y_moves, x_moves, x_relays, x_fwd, core_moves, own_moves = {}, {}, {}, {}, {}, {}
-    reduce_moves, b_moves, b_relays, b_fwd, yb_moves, zb_moves = {}, {}, {}, {}, {}, {}
+    q_moves, p_moves, f_moves, x_moves, core_moves, own_moves = {}, {}, {}, {}, {}, {}
+    reduce_moves, b_moves, yb_moves, zb_moves = {}, {}, {}, {}
+    n_rows = N_Y * ROWS
+
+    def to_planes(key, src, dst):
+        moves = [remote(src((y + s) % N_Y), dst, along_y(s)) for s in (2, 1, 3)]
+        own_moves[key] = local(src(y), dst)
+        return moves
 
     def d1(c):
         slots(c)
-        both = toks[c].reshape(2 * n_tok, feat)
-        rows = jnp.dot(picks[...], both, preferred_element_type=F32).astype(BF16)
-        g_buf[c] = rows.reshape(N_Y, N_LO, ROWS, feat)
-        y_moves[c] = [
-            remote(g_buf.at[c, (y + s) % N_Y], y_in.at[c, :, y], along_y(s)) for s in (2, 1, 3)
-        ]
-        own_moves[c] = local(g_buf.at[c, y], y_in.at[c, :, y])
-
-    half = N_Y // 2
+        both = toks[c, hi].reshape(2 * n_tok, feat)
+        rows = jnp.dot(picks[c], both, preferred_element_type=F32).astype(BF16)
+        g_buf[c] = rows.reshape(N_LO, N_Y, ROWS, feat)
+        q_moves[c] = to_planes((c, "q"), lambda t: g_buf.at[c, 1 - lo, t], y_in.at[c, y])
+
+    def d1p(c):
+        p_moves[c] = to_planes((c, "p"), lambda t: g_buf.at[c, lo, t], x_buf.at[c, hi, core, lo, y])
+
+    def d1f(c):
+        both = toks[c, 1 - hi].reshape(2 * n_tok, feat)
+        at = pl.ds(pl.multiple_of(lo * n_rows, n_rows), n_rows)
+        rows = jnp.dot(picks[c, at, :], both, preferred_element_type=F32).astype(BF16)
+        g_far[c] = rows.reshape(N_Y, ROWS, feat)
+        f_moves[c] = to_planes((c, "f"), lambda t: g_far.at[c, t], x_buf.at[c, 1 - hi, core, lo, y])
 
     def d2(c):
-        own_moves[c].wait()
-        received(y_moves[c])
-        mine = y_in.at[c, lo]
-        x_relays[c] = [
-            remote(mine.at[pl.ds(0, half)], relay.at[c, 0], along_x(1)),
-            remote(mine.at[pl.ds(half, half)], relay.at[c, 1], along_x(3)),
-        ]
-        x_moves[c] = [
-            remote(y_in.at[c, 1 - lo], x_buf.at[c, hi, core, lo], along_x(1)),
-            remote(y_in.at[c, 1 - lo], x_buf.at[c, hi, core, lo], along_x(3)),
-        ]
-        core_moves[c] = [remote(mine, x_buf.at[c, hi, core, lo], partner)]
-        own_moves[c] = local(mine, x_buf.at[c, hi, core, lo])
+        own_moves[c, "q"].wait()
+        received(q_moves[c])
+        dst = x_buf.at[c, hi, core, lo]
+        x_moves[c] = [remote(y_in.at[c], dst, along_x(1)), remote(y_in.at[c], dst, along_x(3))]
 
     def d3(c):
-        received(x_relays[c])
-        x_fwd[c] = [
-            remote(relay.at[c, 0], x_buf.at[c, left // N_LO, core, 1 - lo, pl.ds(0, half)], along_x(1)),
-            remote(relay.at[c, 1], x_buf.at[c, right // N_LO, core, 1 - lo, pl.ds(half, half)], along_x(3)),
-        ]
+        own_moves[c, "p"].wait()
+        received(p_moves[c])
+        near = x_buf.at[c, hi, core, lo]
+        core_moves.setdefault(c, []).append(remote(near, near, partner))
+        own_moves[c, "f"].wait()
+        received(f_moves[c])
+        far = x_buf.at[c, 1 - hi, core, lo]
+        core_moves[c].append(remote(far, far, partner))
 
     def d4(c):
         received(x_moves[c])
         for other in (left, right):
             block = x_buf.at[c, other // N_LO, core, 1 - lo]
-            core_moves[c].append(remote(block, block, partner))
-        received(x_fwd[c])
-        block = x_buf.at[c, across // N_LO, core, lo]
-        core_moves[c].append(remote(block, block, partner))
+            core_moves.setdefault(c, []).append(remote(block, block, partner))
 
     def d5(c):
-        own_moves[c].wait()
         received(core_moves[c])
         sent(core_moves[c])
 
@@ -252,53 +268,62 @@
             return carry
 
         lax.fori_loop(0, N_HI * N_LO * N_Y, add, 0)
-        far = x_buf.at[c, across // N_LO, core, lo]
-        b_relays[c] = [
-            remote(far.at[pl.ds(0, half)], relay_back.at[c, 0], along_x(1)),
-            remote(far.at[pl.ds(half, half)], relay_back.at[c, 1], along_x(3)),
+        for p, f in enumerate(pieces(c)):
+            b_moves[c, p] = [
+                remote(
+                    x_buf.at[c, other // N_LO, core, par, :, :, f], x_back.at[c, i, :, :, f], along_x(step)
+                )
+                for i, (other, par, step) in enumerate(
+                    ((right, 1 - lo, 1), (left, 1 - lo, 3), (across, lo, 2))
+                )
+            ]
+
+    def pieces(c):
+        if PIECES[c] == 1:
+            return [pl.ds(0, feat)]
+        cut = (feat // 2 + 127) // 128 * 128
+        return [pl.ds(0, cut), pl.ds(cut, feat - cut)]
+
+    def r3(c, p):
+        f = pieces(c)[p]
+        received(b_moves[c, p])
+
+        def add(i, carry):
+            side = x_back[c, 0, i, :, f].astype(F32) + x_back[c, 1, i, :, f].astype(F32)
+            y_out[c, 1 - lo, i, :, f] = side.astype(BF16)
+            same = x_buf[c, hi, core, lo, i, :, f].astype(F32) + x_back[c, 2, i, :, f].astype(F32)
+            y_out[c, lo, i, :, f] = same.astype(BF16)
+            return carry
+
+        lax.fori_loop(0, N_Y, add, 0)
+        yb_moves[c, p] = [
+            remote(y_out.at[c, :, (y + s) % N_Y, :, f], y_back.at[c, :, y, :, f], along_y(s))
+            for s in (2, 1, 3)
         ]
-        b_moves[c] = [
-            remote(x_buf.at[c, right // N_LO, core, 1 - lo], x_back.at[c, 0], along_x(1)),
-            remote(x_buf.at[c, left // N_LO, core, 1 - lo], x_back.at[c, 1], along_x(3)),
-        ]
-
-    def r2(c):
-        received(b_relays[c])
-        b_fwd[c] = [
-            remote(relay_back.at[c, 0], x_back.at[c, 2, pl.ds(0, half)], along_x(1)),
-            remote(relay_back.at[c, 1], x_back.at[c, 2, pl.ds(half, half)], along_x(3)),
-        ]
-
-    def r3(c):
-        received(b_moves[c])
-        received(b_fwd[c])
-
-        def add(i, carry):
-            y_out[c, 1 - lo, i] = (x_back[c, 0, i].astype(F32) + x_back[c, 1, i].astype(F32)).astype(BF16)
-            y_out[c, lo, i] = (x_buf[c, hi, core, lo, i].astype(F32) + x_back[c, 2, i].astype(F32)).astype(BF16)
-            return carry
-
-        lax.fori_loop(0, N_Y, add, 0)
-        yb_moves[c] = [
-            remote(y_out.at[c, :, (y + s) % N_Y], y_back.at[c, y], along_y(s)) for s in (2, 1, 3)
-        ]
-        own_moves[c] = local(y_out.at[c, :, y], y_back.at[c, y])
-
-    def r4(c):
-        own_moves[c].wait()
-        received(yb_moves[c])
-        rows = y_back[c].reshape(N_Y * N_LO * ROWS, feat)
+        own_back[c, p] = local(y_out.at[c, :, y, :, f], y_back.at[c, :, y, :, f])
+
+    def r4(c, p):
+        f = pieces(c)[p]
+        own_back[c, p].wait()
+        received(yb_moves[c, p])
+        rows = y_back[c, :, :, :, f]
+        rows = rows.reshape(N_Y * N_LO * ROWS, rows.shape[-1])
         dims = (((0,), (0,)), ((), ()))
         total = lax.dot_general(mix_hi[c], rows, dims, preferred_element_type=F32)
         total = total + lax.dot_general(mix_lo[c], rows, dims, preferred_element_type=F32)
-        z_out[c] = total.astype(BF16).reshape(2, n_tok, feat)
+        z_out[c, :, :, f] = total.astype(BF16).reshape(2, n_tok, rows.shape[-1])
         for j, d in enumerate(CHUNKS[c]):
+            src, dst = z_out.at[c, j, :, f], z_back.at[c, j, :, f]
             if d:
-                zb_moves[c, j] = remote(z_out.at[c, j], z_back.at[c, j], along_z(d))
+                zb_moves[c, j, p] = remote(src, dst, along_z(d))
             else:
-                own_z.append(local(z_out.at[c, j], z_back.at[c, j]))
-
-    own_z = []
+                own_z.append(local(src, dst))
+
+    own_z, own_back = [], {}
+
+    def own():
+        for load in own_loads:
+            load.wait()
 
     def load_weights():
         for load in weight_loads:
@@ -320,53 +345,67 @@
 
         lax.fori_loop(0, hidden // 16, pick_down, 0)
 
-    z_forward(0)
-    z_forward(1)
-    z_forward(-1)
-    for load in own_loads:
-        load.wait()
+    swap()
+    z_near(0)
+    z_near(1)
+    z_near(-1)
     d1(0)
+    z_far(0)
     load_weights()
-    z_forward(2)
-    z_forward(-2)
     d2(0)
-    z_forward(3)
-    z_forward(-3)
+    d1p(0)
+    z_near(2)
+    z_near(-2)
     d1(1)
+    z_far(1)
+    z_far(-1)
+    d1f(0)
+    d2(1)
+    d1p(1)
+    d4(0)
     d3(0)
-    z_forward(4)
+    z_near(3)
+    z_near(-3)
+    z_far(2)
+    z_far(-2)
     d1(2)
-    d2(1)
-    d4(0)
-    d1(3)
-    d3(1)
+    d1f(1)
     d5(0)
     d2(2)
+    d1p(2)
+    r1(0)
+    z_near(4)
+    own()
+    d1(3)
+    z_far(3)
+    z_far(-3)
+    d1f(2)
+    d3(1)
     d4(1)
-    r1(0)
-    d3(2)
     d5(1)
     d2(3)
+    d1p(3)
+    r1(1)
+    z_far(4)
+    d1f(3)
+    d3(2)
     d4(2)
-    r1(1)
-    r2(0)
+    r3(0, 0)
+    d5(2)
+    r4(0, 0)
+    r1(2)
     d3(3)
-    d5(2)
-    r3(0)
     d4(3)
-    r1(2)
-    r2(1)
     d5(3)
+    r3(1, 0)
     r1(3)
-    r2(2)
-    r3(1)
-    r4(0)
-    r2(3)
-    r3(2)
-    r4(1)
-    r3(3)
-    r4(2)
-    r4(3)
+    r4(1, 0)
+    r3(2, 0)
+    r4(2, 0)
+    r3(3, 0)
+    r4(3, 0)
+    r3(3, 1)
+    r4(3, 1)
     for copy in own_z:
         copy.wait()
     received(zb_moves.values())
@@ -384,8 +423,8 @@
     sent(list(started))
 
 
-N_REMOTE = 14 + 4 * (3 + 6 + 4 + 1 + 6 + 3) + 7
-N_LOCAL = 5 + 4 * 3 + 1
+N_REMOTE = 22 + 4 * (9 + 2 + 4 + 1) + 5 * (3 + 3) + 8
+N_LOCAL = 4 + 4 * 3 + 5 + 2
 
 
 def per_device(tokens, expert_ids, gate_weights, replica_plan, w_gate, w_up, w_down):
@@ -394,7 +433,6 @@
     tok, feat = tokens.shape
     width = w_gate.shape[1]
     hidden = w_gate.shape[2]
-    meta = jnp.concatenate([expert_ids.T.astype(F32), gate_weights.T], axis=0)
     n_chunk = len(CHUNKS)
     vmem = pl.BlockSpec(memory_space=pltpu.VMEM)
     hbm = pl.BlockSpec(memory_space=pl.ANY)
@@ -403,26 +441,26 @@
     return pl.pallas_call(
         functools.partial(kernel, n_z),
         out_shape=jax.ShapeDtypeStruct((tok, feat), BF16),
-        in_specs=[vmem, vmem, pl.BlockSpec(memory_space=pltpu.SMEM), hbm, hbm, hbm],
+        in_specs=[vmem, vmem, vmem, pl.BlockSpec(memory_space=pltpu.SMEM), hbm, hbm, hbm],
         out_specs=vmem,
         scratch_shapes=[
             pltpu.VMEM((3, width, hidden), BF16),
             pltpu.VMEM((3, width, hidden), BF16),
             pltpu.VMEM((3, hidden, width), BF16),
-            pltpu.VMEM((n_chunk, 2, tok, feat), BF16),
+            pltpu.VMEM((n_chunk, N_HI, 2, tok, feat), BF16),
             pltpu.VMEM((n_chunk, 2, 16, tok), F32),
-            pltpu.VMEM((slot_rows, 2 * tok), BF16),
+            pltpu.VMEM((16, tok), F32),
             pltpu.VMEM((n_chunk, slot_rows, 2 * tok), BF16),
             pltpu.VMEM((n_chunk, slot_rows, 2 * tok), BF16),
-            pltpu.VMEM((n_chunk, N_Y, N_LO, ROWS, feat), BF16),
+            pltpu.VMEM((n_chunk, slot_rows, 2 * tok), BF16),
             pltpu.VMEM((n_chunk, N_LO) + block, BF16),
+            pltpu.VMEM((n_chunk,) + block, BF16),
+            pltpu.VMEM((n_chunk,) + block, BF16),
             pltpu.VMEM((n_chunk, N_HI, N_CORE, N_LO) + block, BF16),
-            pltpu.VMEM((n_chunk, 2, N_Y // 2, ROWS, feat), BF16),
             pltpu.VMEM((n_chunk, N_HI, N_LO) + block, BF16),
             pltpu.VMEM((n_chunk, 3) + block, BF16),
-            pltpu.VMEM((n_chunk, 2, N_Y // 2, ROWS, feat), BF16),
             pltpu.VMEM((n_chunk, N_LO) + block, BF16),
-            pltpu.VMEM((n_chunk, N_Y, N_LO, ROWS, feat), BF16),
+            pltpu.VMEM((n_chunk, N_LO) + block, BF16),
             pltpu.VMEM((n_chunk, 2, tok, feat), BF16),
             pltpu.VMEM((n_chunk, 2, tok, feat), BF16),
             pltpu.SemaphoreType.DMA((N_REMOTE,)),
@@ -432,7 +470,7 @@
         compiler_params=pltpu.CompilerParams(
             collective_id=0, has_side_effects=True, vmem_limit_bytes=67043328
         ),
-    )(tokens, meta, replica_plan, w_gate, w_up, w_down)
+    )(tokens, expert_ids.T, gate_weights.T, replica_plan, w_gate, w_up, w_down)
 
 
 def solution(mesh):

time: 193 us -> 144 us (0.75)
  Pallas kernels: 189 us -> 140 us
  other arithmetic: 1.97 us -> 0 us
    pallas_call x1, Pallas kernels: 189 us -> 140 us  [per_device(): pl.pallas_call(functools.partial(kernel, n_z), out_shape=jax.ShapeDtypeSt...]
where the time goes in v3:
time: 144 us; the launch traced here: 142 us
  Pallas kernels  140 us (97%)
  local copies, waits for them, and re-layouts  1.65 us (1%)
    pallas_call x1, Pallas kernels, per_device(): pl.pallas_call(functools.partial(kernel, n_z), out_shape=jax.ShapeDtypeSt...  140 us

profile of v3, /device:TPU:2, one launch (start us, length us, event | category | flops | bytes accessed | tf_op | source)
XLA Modules:
  0.0 142.1 jit_solution(2320761854790328323)
XLA Ops:
  0.0 140.4 %shard_map.73 = bf16[128,896]{1,0:T(8,128)(2,1)} custom-call(bf16[128,896]{1,0:T(8,128)(2,1)} %tok_ref.1, s32[8,128]{1,0:T(8,128)} %bitcast.2, f32[8,128]{1,0:T(8,128)} %bitcast.3, s32[64]{0:T(128)} %plan_ref.1, bf16[2,3584,256]{2,1,0:T(8,128)(2,1)} %wg_hbm.1, bf16[2,3584,256]{2,1,0:T(8,128)(2,1)} %wu_hbm.1, bf16[2,256,3584]{2,1,0:T(8,128)(2,1)} %wd_hbm.1), custom_call_target="tpu_custom_call" | custom-call | tf_op jit(solution)/shard_map/pallas_call | solution.py:441
  140.4 1.6 %copy.9 = bf16[128,896]{1,0:T(8,128)(2,1)} copy(bf16[128,896]{1,0:T(8,128)(2,1)} %shard_map.73) | data formatting | bytes 458752

commit v4 on v3

--- a/solution.py
+++ b/solution.py
@@ -13,7 +13,7 @@
 GROUPS = 3
 ROWS = GROUPS * 2 * CAP
 CHUNKS = ((1, -1), (2, -2), (3, -3), (0, 4))
-PIECES = (1, 1, 1, 2)
+PIECES = (2, 3, 2, 2)
 BF16, F32 = jnp.bfloat16, jnp.float32
 
 
@@ -279,10 +279,10 @@
             ]
 
     def pieces(c):
-        if PIECES[c] == 1:
-            return [pl.ds(0, feat)]
-        cut = (feat // 2 + 127) // 128 * 128
-        return [pl.ds(0, cut), pl.ds(cut, feat - cut)]
+        tiles = feat // 128
+        ends = [-(-tiles * (i + 1) // PIECES[c]) for i in range(PIECES[c])]
+        starts = [0] + ends[:-1]
+        return [pl.ds(128 * i, 128 * (j - i)) for i, j in zip(starts, ends)]
 
     def r3(c, p):
         f = pieces(c)[p]
@@ -345,67 +345,75 @@
 
         lax.fori_loop(0, hidden // 16, pick_down, 0)
 
+    z_near(0)
     swap()
-    z_near(0)
     z_near(1)
     z_near(-1)
     d1(0)
+    z_near(-2)
+    z_near(2)
+    d1(1)
+    d1p(0)
+    d2(0)
+    load_weights()
     z_far(0)
-    load_weights()
-    d2(0)
-    d1p(0)
-    z_near(2)
-    z_near(-2)
-    d1(1)
+    own()
+    z_near(3)
+    d2(1)
+    z_near(-3)
+    d1(2)
+    z_far(-1)
     z_far(1)
-    z_far(-1)
     d1f(0)
-    d2(1)
-    d1p(1)
+    d2(2)
+    z_near(4)
+    d1(3)
+    d3(0)
     d4(0)
-    d3(0)
-    z_near(3)
-    z_near(-3)
+    z_far(-2)
+    d1p(2)
     z_far(2)
-    z_far(-2)
-    d1(2)
-    d1f(1)
+    d2(3)
     d5(0)
-    d2(2)
-    d1p(2)
+    z_far(-3)
+    z_far(3)
+    d1f(2)
+    d4(1)
+    d1p(3)
     r1(0)
-    z_near(4)
-    own()
-    d1(3)
-    z_far(3)
-    z_far(-3)
-    d1f(2)
-    d3(1)
-    d4(1)
-    d5(1)
-    d2(3)
-    d1p(3)
-    r1(1)
+    d4(3)
+    d4(2)
+    d3(2)
     z_far(4)
     d1f(3)
-    d3(2)
-    d4(2)
+    d1f(1)
+    d5(2)
+    d1p(1)
     r3(0, 0)
-    d5(2)
-    r4(0, 0)
     r1(2)
     d3(3)
-    d4(3)
+    r3(0, 1)
     d5(3)
+    r4(0, 1)
+    r3(2, 0)
+    d3(1)
+    r4(0, 0)
+    r1(3)
+    d5(1)
+    r3(2, 1)
+    r4(2, 0)
+    r4(2, 1)
+    r1(1)
+    r3(3, 0)
+    r3(3, 1)
+    r4(3, 0)
+    r4(3, 1)
     r3(1, 0)
-    r1(3)
+    r3(1, 1)
     r4(1, 0)
-    r3(2, 0)
-    r4(2, 0)
-    r3(3, 0)
-    r4(3, 0)
-    r3(3, 1)
-    r4(3, 1)
+    r3(1, 2)
+    r4(1, 1)
+    r4(1, 2)
     for copy in own_z:
         copy.wait()
     received(zb_moves.values())
@@ -423,8 +431,10 @@
     sent(list(started))
 
 
-N_REMOTE = 22 + 4 * (9 + 2 + 4 + 1) + 5 * (3 + 3) + 8
-N_LOCAL = 4 + 4 * 3 + 5 + 2
+N_REMOTE = 22 + 4 * (9 + 2 + 4 + 1) + sum(
+    n * (6 + sum(d != 0 for d in pair)) for n, pair in zip(PIECES, CHUNKS)
+)
+N_LOCAL = 4 + 4 * 3 + sum(n * (1 + (0 in pair)) for n, pair in zip(PIECES, CHUNKS))
 
 
 def per_device(tokens, expert_ids, gate_weights, replica_plan, w_gate, w_up, w_down):

time: 144 us -> 133 us (0.924)
  Pallas kernels: 140 us -> 130 us
    pallas_call x1, Pallas kernels: 140 us -> 130 us  [per_device(): pl.pallas_call(functools.partial(kernel, n_z), out_shape=jax.ShapeDtypeSt...]
where the time goes in v4:
time: 133 us; the launch traced here: 132 us
  Pallas kernels  130 us (98%)
  local copies, waits for them, and re-layouts  1.65 us (1%)
    pallas_call x1, Pallas kernels, per_device(): pl.pallas_call(functools.partial(kernel, n_z), out_shape=jax.ShapeDtypeSt...  130 us

profile of v4, /device:TPU:2, one launch (start us, length us, event | category | flops | bytes accessed | tf_op | source)
XLA Modules:
  0.0 131.7 jit_solution(8433588570906901401)
XLA Ops:
  0.0 130.1 %shard_map.73 = bf16[128,896]{1,0:T(8,128)(2,1)} custom-call(bf16[128,896]{1,0:T(8,128)(2,1)} %tok_ref.1, s32[8,128]{1,0:T(8,128)} %bitcast.2, f32[8,128]{1,0:T(8,128)} %bitcast.3, s32[64]{0:T(128)} %plan_ref.1, bf16[2,3584,256]{2,1,0:T(8,128)(2,1)} %wg_hbm.1, bf16[2,3584,256]{2,1,0:T(8,128)(2,1)} %wu_hbm.1, bf16[2,256,3584]{2,1,0:T(8,128)(2,1)} %wd_hbm.1), custom_call_target="tpu_custom_call" | custom-call | tf_op jit(solution)/shard_map/pallas_call | solution.py:451
  130.1 1.6 %copy.9 = bf16[128,896]{1,0:T(8,128)(2,1)} copy(bf16[128,896]{1,0:T(8,128)(2,1)} %shard_map.73) | data formatting | bytes 458752

commit v5 on v4

--- a/solution.py
+++ b/solution.py
@@ -14,13 +14,15 @@
 ROWS = GROUPS * 2 * CAP
 CHUNKS = ((1, -1), (2, -2), (3, -3), (0, 4))
 PIECES = (2, 3, 2, 2)
+DIRECT = (0,)
+MERGE = ()
 BF16, F32 = jnp.bfloat16, jnp.float32
 
 
 def kernel(
     n_z, tok_ref, ids_ref, gate_ref, plan_ref, wg_hbm, wu_hbm, wd_hbm, out_ref,
     wg, wu, wd, toks, metas, meta_own, picks, mix_hi, mix_lo, g_buf, g_far, y_in, x_buf, core_in,
-    x_back, y_out, y_back, z_out, z_back,
+    x_back, y_out, y_back, z_out, z_back, far_back, far_out, far_in, merged, swap_out, swap_in,
     send_sem, recv_sem, local_sem,
 ):
     expert = lax.axis_index("expert")
@@ -274,7 +276,7 @@
                     x_buf.at[c, other // N_LO, core, par, :, :, f], x_back.at[c, i, :, :, f], along_x(step)
                 )
                 for i, (other, par, step) in enumerate(
-                    ((right, 1 - lo, 1), (left, 1 - lo, 3), (across, lo, 2))
+                    ((right, 1 - lo, 1), (left, 1 - lo, 3), (across, lo, 2))[: 2 if c in DIRECT else 3]
                 )
             ]
 
@@ -291,8 +293,10 @@
         def add(i, carry):
             side = x_back[c, 0, i, :, f].astype(F32) + x_back[c, 1, i, :, f].astype(F32)
             y_out[c, 1 - lo, i, :, f] = side.astype(BF16)
-            same = x_buf[c, hi, core, lo, i, :, f].astype(F32) + x_back[c, 2, i, :, f].astype(F32)
-            y_out[c, lo, i, :, f] = same.astype(BF16)
+            same = x_buf[c, hi, core, lo, i, :, f]
+            if c not in DIRECT:
+                same = (same.astype(F32) + x_back[c, 2, i, :, f].astype(F32)).astype(BF16)
+            y_out[c, lo, i, :, f] = same
             return carry
 
         lax.fori_loop(0, N_Y, add, 0)
@@ -300,26 +304,77 @@
             remote(y_out.at[c, :, (y + s) % N_Y, :, f], y_back.at[c, :, y, :, f], along_y(s))
             for s in (2, 1, 3)
         ]
-        own_back[c, p] = local(y_out.at[c, :, y, :, f], y_back.at[c, :, y, :, f])
+        own_back[c, p] = [local(y_out.at[c, :, y, :, f], y_back.at[c, :, y, :, f])]
+        if c in DIRECT:
+            n = DIRECT.index(c)
+            src = x_buf.at[c, 1 - hi, core, lo]
+            yb_moves[c, p] += [
+                remote(src.at[(y + s) % N_Y, :, f], far_back.at[n, y, :, f], along_y(s)) for s in (2, 1, 3)
+            ]
+            own_back[c, p].append(local(src.at[y, :, f], far_back.at[n, y, :, f]))
 
     def r4(c, p):
         f = pieces(c)[p]
-        own_back[c, p].wait()
+        for copy in own_back[c, p]:
+            copy.wait()
         received(yb_moves[c, p])
         rows = y_back[c, :, :, :, f]
         rows = rows.reshape(N_Y * N_LO * ROWS, rows.shape[-1])
         dims = (((0,), (0,)), ((), ()))
         total = lax.dot_general(mix_hi[c], rows, dims, preferred_element_type=F32)
         total = total + lax.dot_general(mix_lo[c], rows, dims, preferred_element_type=F32)
-        z_out[c, :, :, f] = total.astype(BF16).reshape(2, n_tok, rows.shape[-1])
+        total = total.reshape(2, n_tok, rows.shape[-1])
         for j, d in enumerate(CHUNKS[c]):
-            src, dst = z_out.at[c, j, :, f], z_back.at[c, j, :, f]
-            if d:
-                zb_moves[c, j, p] = remote(src, dst, along_z(d))
+            behind = d + (1 if d > 0 else -1)
+            part = total[j]
+            if d and behind in MERGE:
+                if p == 0:
+                    received(m_moves[behind])
+                part = part + merged[MERGE.index(behind), :, f].astype(F32)
+            z_out[c, j, :, f] = part.astype(BF16)
+            src = z_out.at[c, j, :, f]
+            if d in MERGE:
+                step = 1 if d > 0 else -1
+                m_moves.setdefault(d, []).append(
+                    remote(src, merged.at[MERGE.index(d), :, f], along_z(step))
+                )
+            elif d:
+                zb_moves[c, j, p] = remote(src, z_back.at[c, j, :, f], along_z(d))
             else:
-                own_z.append(local(src, dst))
-
-    own_z, own_back = [], {}
+                own_z.append(local(src, z_back.at[c, j, :, f]))
+        if c in DIRECT:
+            n = DIRECT.index(c)
+            at = pl.ds(pl.multiple_of(lo * n_rows, n_rows), n_rows)
+            rows = far_back[n, :, :, f]
+            rows = rows.reshape(n_rows, rows.shape[-1])
+            total = lax.dot_general(mix_hi[c, at, :], rows, dims, preferred_element_type=F32)
+            total = total + lax.dot_general(mix_lo[c, at, :], rows, dims, preferred_element_type=F32)
+            far_out[n, :, :, f] = total.astype(BF16).reshape(2, n_tok, rows.shape[-1])
+            for j, d in enumerate(CHUNKS[c]):
+                src, dst = far_out.at[n, j, :, f], far_in.at[n, j, :, f]
+                if d:
+                    far_moves.append(remote(src, dst, along_z(d)))
+                else:
+                    far_own.append(local(src, dst))
+
+    def fin():
+        received(far_moves)
+        for copy in far_own:
+            copy.wait()
+
+        def add(i, carry):
+            at = pl.ds(pl.multiple_of(i * 16, 16), 16)
+            total = jnp.zeros((16, feat), F32)
+            for n in range(len(DIRECT)):
+                for j in range(2):
+                    total = total + far_in[n, j, at, :].astype(F32)
+            swap_out[at, :] = total.astype(BF16)
+            return carry
+
+        lax.fori_loop(0, n_tok // 16, add, 0)
+        swap_moves.append(remote(swap_out, swap_in, along_x(2)))
+
+    own_z, own_back, m_moves, far_moves, far_own, swap_moves = [], {}, {}, [], [], []
 
     def own():
         for load in own_loads:
@@ -345,69 +400,70 @@
 
         lax.fori_loop(0, hidden // 16, pick_down, 0)
 
+    swap()
     z_near(0)
-    swap()
+    z_near(-1)
     z_near(1)
-    z_near(-1)
     d1(0)
+    z_far(0)
+    d2(0)
+    d1p(0)
+    z_near(2)
     z_near(-2)
-    z_near(2)
     d1(1)
-    d1p(0)
-    d2(0)
+    z_far(1)
+    z_far(-1)
+    d1f(0)
     load_weights()
-    z_far(0)
     own()
+    z_near(-3)
     z_near(3)
+    d4(0)
+    d1(2)
     d2(1)
-    z_near(-3)
-    d1(2)
-    z_far(-1)
-    z_far(1)
-    d1f(0)
+    d1p(1)
+    d3(0)
     d2(2)
+    d1p(2)
+    z_far(2)
+    z_far(-2)
+    d5(0)
     z_near(4)
     d1(3)
-    d3(0)
-    d4(0)
-    z_far(-2)
-    d1p(2)
-    z_far(2)
-    d2(3)
-    d5(0)
+    r1(0)
     z_far(-3)
     z_far(3)
     d1f(2)
+    d4(2)
+    d1f(1)
     d4(1)
-    d1p(3)
-    r1(0)
-    d4(3)
-    d4(2)
     d3(2)
+    d2(3)
     z_far(4)
     d1f(3)
-    d1f(1)
+    d1p(3)
+    r3(0, 0)
     d5(2)
-    d1p(1)
-    r3(0, 0)
     r1(2)
+    r3(0, 1)
+    d4(3)
     d3(3)
-    r3(0, 1)
     d5(3)
-    r4(0, 1)
+    r4(0, 0)
     r3(2, 0)
     d3(1)
-    r4(0, 0)
     r1(3)
-    d5(1)
+    r4(0, 1)
     r3(2, 1)
     r4(2, 0)
-    r4(2, 1)
+    d5(1)
     r1(1)
     r3(3, 0)
+    r4(2, 1)
     r3(3, 1)
     r4(3, 0)
     r4(3, 1)
+    fin()
     r3(1, 0)
     r3(1, 1)
     r4(1, 0)
@@ -417,13 +473,15 @@
     for copy in own_z:
         copy.wait()
     received(zb_moves.values())
+    received(swap_moves)
 
     def finish(i, carry):
         at = pl.ds(pl.multiple_of(i * 16, 16), 16)
-        total = jnp.zeros((16, feat), F32)
+        total = swap_in[at, :].astype(F32) if DIRECT else jnp.zeros((16, feat), F32)
         for c in range(n_chunk):
             for j in range(2):
-                total = total + z_back[c, j, at, :].astype(F32)
+                if CHUNKS[c][j] not in MERGE:
+                    total = total + z_back[c, j, at, :].astype(F32)
         out_ref[at, :] = total.astype(out_ref.dtype)
         return carry
 
@@ -431,10 +489,13 @@
     sent(list(started))
 
 
-N_REMOTE = 22 + 4 * (9 + 2 + 4 + 1) + sum(
-    n * (6 + sum(d != 0 for d in pair)) for n, pair in zip(PIECES, CHUNKS)
-)
-N_LOCAL = 4 + 4 * 3 + sum(n * (1 + (0 in pair)) for n, pair in zip(PIECES, CHUNKS))
+N_REMOTE = 23 + 4 * (9 + 2 + 4 + 1)
+N_LOCAL = 4 + 4 * 3
+for _c, _pair in enumerate(CHUNKS):
+    _far = 1 + (_c in DIRECT)
+    _away = sum(_d != 0 for _d in _pair)
+    N_REMOTE += PIECES[_c] * (2 + (_c not in DIRECT) + _far * (3 + _away))
+    N_LOCAL += PIECES[_c] * _far * (1 + (0 in _pair))
 
 
 def per_device(tokens, expert_ids, gate_weights, replica_plan, w_gate, w_up, w_down):
@@ -473,6 +534,12 @@
             pltpu.VMEM((n_chunk, N_LO) + block, BF16),
             pltpu.VMEM((n_chunk, 2, tok, feat), BF16),
             pltpu.VMEM((n_chunk, 2, tok, feat), BF16),
+            pltpu.VMEM((max(len(DIRECT), 1),) + block, BF16),
+            pltpu.VMEM((max(len(DIRECT), 1), 2, tok, feat), BF16),
+            pltpu.VMEM((max(len(DIRECT), 1), 2, tok, feat), BF16),
+            pltpu.VMEM((max(len(MERGE), 1), tok, feat), BF16),
+            pltpu.VMEM((tok, feat), BF16),
+            pltpu.VMEM((tok, feat), BF16),
             pltpu.SemaphoreType.DMA((N_REMOTE,)),
             pltpu.SemaphoreType.DMA((N_REMOTE,)),
             pltpu.SemaphoreType.DMA((N_LOCAL,)),

time: 133 us -> 129 us (0.970)
  Pallas kernels: 130 us -> 127 us
    pallas_call x1, Pallas kernels: 130 us -> 127 us  [per_device(): pl.pallas_call(functools.partial(kernel, n_z), out_shape=jax.ShapeDtypeSt...]
where the time goes in v5:
time: 129 us; the launch traced here: 128 us
  Pallas kernels  127 us (98%)
  local copies, waits for them, and re-layouts  1.65 us (1%)
    pallas_call x1, Pallas kernels, per_device(): pl.pallas_call(functools.partial(kernel, n_z), out_shape=jax.ShapeDtypeSt...  127 us

profile of v5, /device:TPU:2, one launch (start us, length us, event | category | flops | bytes accessed | tf_op | source)
XLA Modules:
  0.0 128.3 jit_solution(18041760457414152740)
XLA Ops:
  0.0 126.6 %shard_map.73 = bf16[128,896]{1,0:T(8,128)(2,1)} custom-call(bf16[128,896]{1,0:T(8,128)(2,1)} %tok_ref.1, s32[8,128]{1,0:T(8,128)} %bitcast.2, f32[8,128]{1,0:T(8,128)} %bitcast.3, s32[64]{0:T(128)} %plan_ref.1, bf16[2,3584,256]{2,1,0:T(8,128)(2,1)} %wg_hbm.1, bf16[2,3584,256]{2,1,0:T(8,128)(2,1)} %wu_hbm.1, bf16[2,256,3584]{2,1,0:T(8,128)(2,1)} %wd_hbm.1), custom_call_target="tpu_custom_call" | custom-call | tf_op jit(solution)/shard_map/pallas_call | solution.py:512
  126.6 1.6 %copy.9 = bf16[128,896]{1,0:T(8,128)(2,1)} copy(bf16[128,896]{1,0:T(8,128)(2,1)} %shard_map.73) | data formatting | bytes 458752

commit v6 on v5

--- a/solution.py
+++ b/solution.py
@@ -14,8 +14,8 @@
 ROWS = GROUPS * 2 * CAP
 CHUNKS = ((1, -1), (2, -2), (3, -3), (0, 4))
 PIECES = (2, 3, 2, 2)
-DIRECT = (0,)
-MERGE = ()
+DIRECT = (0, 3, )
+MERGE = (3, -3, 4, )
 BF16, F32 = jnp.bfloat16, jnp.float32
 
 
@@ -402,73 +402,73 @@
 
     swap()
     z_near(0)
+    z_near(1)
     z_near(-1)
-    z_near(1)
     d1(0)
     z_far(0)
     d2(0)
+    z_near(2)
     d1p(0)
-    z_near(2)
+    load_weights()
     z_near(-2)
     d1(1)
+    z_far(-1)
     z_far(1)
-    z_far(-1)
     d1f(0)
-    load_weights()
     own()
     z_near(-3)
     z_near(3)
-    d4(0)
+    d2(1)
     d1(2)
-    d2(1)
+    z_far(2)
     d1p(1)
-    d3(0)
     d2(2)
-    d1p(2)
-    z_far(2)
-    z_far(-2)
-    d5(0)
     z_near(4)
     d1(3)
+    d3(0)
+    d4(0)
+    d4(1)
+    d1p(2)
+    z_far(3)
+    z_far(-2)
+    d2(3)
+    d1p(3)
+    d5(0)
+    z_far(4)
+    d4(2)
+    d1f(3)
+    z_far(-3)
     r1(0)
-    z_far(-3)
-    z_far(3)
     d1f(2)
-    d4(2)
-    d1f(1)
-    d4(1)
-    d3(2)
-    d2(3)
-    z_far(4)
-    d1f(3)
-    d1p(3)
-    r3(0, 0)
-    d5(2)
-    r1(2)
-    r3(0, 1)
     d4(3)
     d3(3)
+    d1f(1)
     d5(3)
-    r4(0, 0)
-    r3(2, 0)
+    r3(0, 0)
+    d3(2)
+    r3(0, 1)
     d3(1)
     r1(3)
+    d5(2)
+    r4(0, 0)
+    r3(3, 0)
+    r1(2)
     r4(0, 1)
+    d5(1)
+    r3(3, 1)
+    r4(3, 0)
+    r3(2, 0)
+    r1(1)
+    r4(3, 1)
     r3(2, 1)
     r4(2, 0)
-    d5(1)
-    r1(1)
-    r3(3, 0)
     r4(2, 1)
-    r3(3, 1)
-    r4(3, 0)
-    r4(3, 1)
-    fin()
     r3(1, 0)
     r3(1, 1)
     r4(1, 0)
     r3(1, 2)
     r4(1, 1)
+    fin()
     r4(1, 2)
     for copy in own_z:
         copy.wait()

time: 129 us -> 126 us (0.977)
  Pallas kernels: 127 us -> 124 us
    pallas_call x1, Pallas kernels: 127 us -> 124 us  [per_device(): pl.pallas_call(functools.partial(kernel, n_z), out_shape=jax.ShapeDtypeSt...]
where the time goes in v6:
time: 126 us; the launch traced here: 125 us
  Pallas kernels  124 us (98%)
  local copies, waits for them, and re-layouts  1.65 us (1%)
    pallas_call x1, Pallas kernels, per_device(): pl.pallas_call(functools.partial(kernel, n_z), out_shape=jax.ShapeDtypeSt...  124 us

profile of v6, /device:TPU:2, one launch (start us, length us, event | category | flops | bytes accessed | tf_op | source)
XLA Modules:
  0.0 125.2 jit_solution(4230540376058450601)
XLA Ops:
  0.0 123.5 %shard_map.73 = bf16[128,896]{1,0:T(8,128)(2,1)} custom-call(bf16[128,896]{1,0:T(8,128)(2,1)} %tok_ref.1, s32[8,128]{1,0:T(8,128)} %bitcast.2, f32[8,128]{1,0:T(8,128)} %bitcast.3, s32[64]{0:T(128)} %plan_ref.1, bf16[2,3584,256]{2,1,0:T(8,128)(2,1)} %wg_hbm.1, bf16[2,3584,256]{2,1,0:T(8,128)(2,1)} %wu_hbm.1, bf16[2,256,3584]{2,1,0:T(8,128)(2,1)} %wd_hbm.1), custom_call_target="tpu_custom_call" | custom-call | tf_op jit(solution)/shard_map/pallas_call | solution.py:512
  123.5 1.6 %copy.9 = bf16[128,896]{1,0:T(8,128)(2,1)} copy(bf16[128,896]{1,0:T(8,128)(2,1)} %shard_map.73) | data formatting | bytes 458752
